TPU v7x, 128 devices: a whole 4x4x4 slice. The times are simulated.
128 devices in a mesh: func: 8 (over z, core), box: 16 (over x, y).
Axes of the slice: x: 4, y: 4, z: 4, core: 2. Of those that a mesh axis runs over, the one named last changes fastest.
Arguments:
- coeffs: bfloat16 [3072, 32, 1024], P(('func', 'box')), may hold values from -8 to 8
- centers: int32 [3072], replicated, may hold values from 0 to 1535, as said below
- kinetic: bfloat16 [1024, 1024], replicated, may hold values from -0.1875 to 0.1875
- potential: float32 [1536, 1024], P(('func', 'box')), may hold values from -1 to 1
Outputs:
- filtered: bfloat16 [3072, 32, 1024], P(('func', 'box'))
- gram_band: float32 [3072, 256], P(('func', 'box'))
Inputs may be any that keep to these rules, and one draw needn't show every extreme that they name: `centers`: centers never fall. The boxes form aligned groups of 32, and the groups aligned blocks of four; every box of a group is the center of the same number of functions, 1, 2 or 4, and each block of four groups holds the numbers 1, 1, 2 and 4 in an order whose running total of (number - 2) stays between -1 and 1. So between 32 and 128 functions touch each box, and some box is touched by exactly 128.
All inputs are finite; a program needn't handle non-finite values.
Results may differ from a plain program's by a relative error of at most 0.0057.
Values may be sent and summed in bfloat16 or wider, within the bound.
A program may use at most 64 MiB of HBM per device.

v0:
```python
import jax
import jax.numpy as jnp
from jax import lax
from jax.experimental import pallas as pl
from jax.experimental.pallas import tpu as pltpu
from jax.sharding import PartitionSpec as P

MESH = pl.DeviceIdType.MESH
BF = jnp.bfloat16
F32 = jnp.float32

SUP = 32
FUN = 24
BOX = 12
RING = 4
OWN = FUN * RING
FRAME = 256
LEFT = 80
SLICE = 256
REACH = 7
BOX_ALL = 1536
FUN_ALL = 3072
VOLUME = 1.0 / (32 * 1024)

FORWARD = (
    (80, 0, 2, 176, -1),
    (144, 2, 2, 48, 1),
    (112, 0, 1, 208, -1),
    (112, 3, 1, 16, 1),
)
NEEDS = (
    ((0, 0), (0, 1), (1, 0), (1, 1)),
    ((3, 3), (3, 2), (2, 3), (2, 2)),
    ((1, 0), (2, 0)),
    ((2, 3), (1, 3)),
)


def exchange_kernel(
    coeffs, pot, meta, y_out, v_out, gram_out,
    frame, slots, back_a, back_b, back_c, back_d, gram, terms, sums, rows_out, rows_in, mixing, potb, boxes,
    y_send, y_recv, x_send, x_recv, v_send, v_recv, s_send, s_recv, c_send, c_recv, bx_send, bx_recv, by_send, by_recv,
):
    me = lax.axis_index("func") * 16 + lax.axis_index("box")
    y = lax.rem(me, RING)
    base = me - y

    def dev(linear):
        wrapped = lax.rem(linear + 128, 128)
        return (lax.div(wrapped, 16), lax.rem(wrapped, 16))

    barrier = pltpu.get_barrier_semaphore()
    for k in range(1, REACH + 1):
        for sign in (1, -1):
            pl.semaphore_signal(barrier, inc=1, device_id=dev(me + sign * k), device_id_type=MESH)

    frame[16:48, 0:3] = jnp.zeros((32, 3, 8, SLICE), BF)
    frame[48:80, 0:2] = jnp.zeros((32, 2, 8, SLICE), BF)
    frame[176:208, 2:4] = jnp.zeros((32, 2, 8, SLICE), BF)
    frame[208:240, 1:4] = jnp.zeros((32, 3, 8, SLICE), BF)
    slots[:, 0:16, :] = jnp.zeros((SUP, 16, SLICE), BF)
    slots[:, 240:256, :] = jnp.zeros((SUP, 16, SLICE), BF)
    potb[0:BOX, :] = pot[...].astype(BF)
    potb[BOX:16, :] = jnp.zeros((16 - BOX, 1024), BF)
    pl.semaphore_wait(barrier, 2 * REACH)

    started = []

    my_rows = pl.ds(pl.multiple_of(LEFT + FUN * y, 8), FUN)
    high = lax.div(y, 2)
    for p in range(4):
        q0 = (0, 1, 3, 2)[p]
        q = q0 + high * (3 - 2 * q0)
        for k in (1, 3, 2):
            yp = lax.rem(y + k, RING)
            copy = pltpu.make_async_remote_copy(
                src_ref=coeffs.at[:, q, :, pl.ds(pl.multiple_of(yp * SLICE, SLICE), SLICE)],
                dst_ref=frame.at[my_rows, q],
                send_sem=y_send.at[k - 1, p],
                recv_sem=y_recv.at[y, q],
                device_id=dev(base + yp),
                device_id_type=MESH,
            )
            copy.start()
            started.append(copy)
        pltpu.make_async_copy(
            coeffs.at[:, q, :, pl.ds(pl.multiple_of(y * SLICE, SLICE), SLICE)],
            frame.at[my_rows, q],
            y_recv.at[y, q],
        ).start()

    v_copies = []
    for o in range(-2, 5):
        if o == 0:
            copy = pltpu.make_async_copy(potb, v_out.at[2], v_recv.at[2])
        else:
            copy = pltpu.make_async_remote_copy(
                src_ref=potb,
                dst_ref=v_out.at[o + 2],
                send_sem=v_send.at[o + 2],
                recv_sem=v_recv.at[o + 2],
                device_id=dev(me - o),
                device_id_type=MESH,
            )
        copy.start()
        v_copies.append(copy)

    arrived = set()

    def wait_piece(ys, q):
        if (ys, q) in arrived:
            return
        arrived.add((ys, q))
        piece = frame.at[pl.ds(LEFT + FUN * ys, FUN), q]
        pltpu.make_async_copy(piece, piece, y_recv.at[ys, q]).wait()

    forwards = []
    for n, (src, q, nq, dst, to) in enumerate(FORWARD):
        for ys, quarter in NEEDS[n]:
            wait_piece(ys, quarter)
        copy = pltpu.make_async_remote_copy(
            src_ref=frame.at[pl.ds(src, 32), pl.ds(q, nq)],
            dst_ref=frame.at[pl.ds(dst, 32), pl.ds(q, nq)],
            send_sem=x_send.at[n],
            recv_sem=x_recv.at[n],
            device_id=dev(me + RING * to),
            device_id_type=MESH,
        )
        copy.start()
        forwards.append(copy)
    for ys in range(RING):
        for q in range(4):
            wait_piece(ys, q)

    row_id = lax.broadcasted_iota(jnp.int32, (FRAME, FRAME), 0)
    col_id = lax.broadcasted_iota(jnp.int32, (FRAME, FRAME), 1)

    def into_slots(pair, carry):
        parts = []
        for half in range(2):
            octet = 2 * pair + half
            select = (row_id == meta[pl.ds(8 + octet, 1), :]).astype(F32).astype(BF)
            raw = frame[pl.ds(pl.multiple_of(8 * octet, 8), 8)]
            raw = raw.astype(F32).reshape(FRAME, SLICE).astype(BF)
            out = jnp.dot(select, raw, preferred_element_type=F32)
            parts.append(out.reshape(SUP, 8, SLICE))
        both = jnp.concatenate(parts, axis=1).astype(BF)
        slots[:, pl.ds(pl.multiple_of(16 * pair, 16), 16), :] = both
        return carry

    lax.fori_loop(5, 11, into_slots, 0)
    for copy in forwards:
        copy.wait_recv()
    lax.fori_loop(1, 5, into_slots, 0)
    lax.fori_loop(11, 15, into_slots, 0)

    rel_row = meta[0:1, :]
    rel_tile = jnp.broadcast_to(rel_row, (FRAME, FRAME))
    rel_col = jnp.sum(
        jnp.where(row_id == col_id, rel_tile.astype(F32), 0.0), axis=1, keepdims=True
    ).astype(jnp.int32)
    low_row = meta[1:2, :]
    top_row = meta[2:3, :]
    boxes[...] = jnp.broadcast_to(rel_col, (FRAME, FRAME))

    def same_box(slot):
        box_row = rel_row + jnp.bitwise_and(slot - rel_row, SUP - 1)
        owned = jnp.logical_and(box_row >= low_row, box_row <= top_row)
        box_row = jnp.where(owned, box_row, -1)
        col = boxes[...]
        box_col = col + jnp.bitwise_and(slot - col, SUP - 1)
        return box_col == box_row

    gram[...] = jnp.zeros((FRAME, FRAME), F32)

    def gram_step(slot, carry):
        held = slots[slot]
        prod = lax.dot_general(held, held, (((1,), (1,)), ((), ())), preferred_element_type=F32)
        gram[...] += jnp.where(same_box(slot), prod, 0.0)
        return carry

    lax.fori_loop(0, SUP, gram_step, 0)
    gram[...] = gram[...] * VOLUME

    s_copies = []

    def send_terms(n, start, slot, target):
        copy = pltpu.make_async_remote_copy(
            src_ref=gram.at[pl.ds(start, FUN)],
            dst_ref=terms.at[slot],
            send_sem=s_send.at[n],
            recv_sem=s_recv.at[slot],
            device_id=dev(target),
            device_id_type=MESH,
        )
        copy.start()
        s_copies.append(copy)

    for k in range(1, 4):
        yp = lax.rem(y + k, RING)
        send_terms(k - 1, pl.multiple_of(LEFT + FUN * yp, 8), 4 + y, base + yp)
    for yp in range(1, 4):
        send_terms(2 + yp, FUN * yp - 16, 8 + y, base - RING + yp)
    for yp in range(0, 3):
        send_terms(6 + yp, 176 + FUN * yp, y, base + RING + yp)

    def wait_terms(slot):
        pltpu.make_async_copy(terms.at[slot], terms.at[slot], s_recv.at[slot]).wait()

    sums[0] = jnp.zeros((FUN, FRAME), F32)
    sums[2] = jnp.zeros((FUN, FRAME), F32)
    sums[1] = gram[my_rows, :]
    for k in range(1, 4):
        slot = 4 + lax.rem(y + k, RING)
        wait_terms(slot)
        sums[1] += terms[slot]

    @pl.when(y <= 2)
    def _():
        for ys in range(RING):
            wait_terms(ys)
        sums[0] = terms[0] + terms[1] + terms[2] + terms[3]

    @pl.when(y >= 1)
    def _():
        for ys in range(RING):
            wait_terms(8 + ys)
        sums[2] = terms[8] + terms[9] + terms[10] + terms[11]

    pad = jnp.zeros((FUN, FRAME), F32)
    wide = jnp.concatenate([sums[0], pad], axis=1)
    wide += pltpu.roll(jnp.concatenate([sums[1], pad], axis=1), 96, 1)
    wide += pltpu.roll(jnp.concatenate([sums[2], pad], axis=1), 192, 1)
    lane = lax.broadcasted_iota(jnp.int32, (FUN, 512), 1)
    sub = lax.broadcasted_iota(jnp.int32, (FUN, 512), 0)
    fixed = (1.5 * (lane == sub + (FUN * y + 176)).astype(F32) - 0.5 * wide)
    rows_out[0] = fixed[:, 0:256].astype(BF)
    rows_out[1] = pltpu.roll(fixed, 512 - 96, 1)[:, 0:256].astype(BF)
    rows_out[2] = pltpu.roll(fixed, 512 - 192, 1)[:, 0:256].astype(BF)

    c_copies = []

    def send_rows(n, which, slot, target):
        copy = pltpu.make_async_remote_copy(
            src_ref=rows_out.at[which],
            dst_ref=rows_in.at[slot],
            send_sem=c_send.at[n],
            recv_sem=c_recv.at[slot],
            device_id=dev(target),
            device_id_type=MESH,
        )
        copy.start()
        return copy

    own_rows = [
        send_rows(k - 1, 1, 4 + y, base + lax.rem(y + k, RING)) for k in range(1, 4)
    ]

    @pl.when(y <= 2)
    def _():
        for yp in range(RING):
            send_rows(3 + yp, 0, 8 + y, base - RING + yp)

    @pl.when(y >= 1)
    def _():
        for yp in range(RING):
            send_rows(7 + yp, 2, y, base + RING + yp)

    band = pltpu.roll(wide, 512 - 49 - FUN * y, 1)
    for bit in range(5):
        moved = pltpu.roll(band, 512 - (1 << bit), 1)
        band = jnp.where(jnp.bitwise_and(sub, 1 << bit) != 0, moved, band)
    gram_out[...] = jnp.where(lane[:, 0:256] == 255, 0.0, band[:, 0:256])

    def wait_rows(slot):
        pltpu.make_async_copy(rows_in.at[slot], rows_in.at[slot], c_recv.at[slot]).wait()

    mixing[0:16, :] = jnp.zeros((16, FRAME), F32)
    mixing[240:256, :] = jnp.zeros((16, FRAME), F32)
    mixing[my_rows, :] = rows_out[1].astype(F32)
    for k in range(1, 4):
        ys = lax.rem(y + k, RING)
        wait_rows(4 + ys)
        mixing[pl.ds(pl.multiple_of(LEFT + FUN * ys, 8), FUN), :] = rows_in[4 + ys].astype(F32)
    for ys in range(0, 3):
        wait_rows(8 + ys)
        mixing[176 + FUN * ys : 200 + FUN * ys, :] = rows_in[8 + ys].astype(F32)
    for ys in range(1, 4):
        wait_rows(ys)
        mixing[FUN * ys - 16 : FUN * ys + 8, :] = rows_in[ys].astype(F32)

    def mix_step(slot, carry):
        mix = jnp.where(same_box(slot), mixing[...], 0.0).astype(BF)
        slots[slot] = jnp.dot(mix, slots[slot], preferred_element_type=F32).astype(BF)
        return carry

    lax.fori_loop(0, SUP, mix_step, 0)

    for copy in forwards:
        copy.wait_send()

    def out_of_slots(pair, carry):
        both = slots[:, pl.ds(pl.multiple_of(16 * pair, 16), 16), :].astype(F32)
        for half in range(2):
            octet = 2 * pair + half
            select = (row_id == meta[pl.ds(40 + octet, 1), :]).astype(F32).astype(BF)
            part = both[:, 8 * half : 8 * half + 8, :].reshape(FRAME, SLICE).astype(BF)
            out = jnp.dot(select, part, preferred_element_type=F32)
            frame[pl.ds(pl.multiple_of(8 * octet, 8), 8)] = out.reshape(8, 4, 8, SLICE).astype(BF)
        return carry

    lax.fori_loop(1, 5, out_of_slots, 0)
    lax.fori_loop(11, 15, out_of_slots, 0)
    backs = (back_a, back_b, back_c, back_d)
    x_backs = []
    for n, (src, q, nq, dst, to) in enumerate(FORWARD):
        copy = pltpu.make_async_remote_copy(
            src_ref=frame.at[pl.ds(dst, 32), pl.ds(q, nq)],
            dst_ref=backs[n],
            send_sem=bx_send.at[n],
            recv_sem=bx_recv.at[n],
            device_id=dev(me - RING * to),
            device_id_type=MESH,
        )
        copy.start()
        x_backs.append(copy)
    lax.fori_loop(5, 11, out_of_slots, 0)
    for n, (src, q, nq, dst, to) in enumerate(FORWARD):
        x_backs[n].wait_recv()
        mine = frame[src : src + 32, q : q + nq].astype(F32)
        frame[src : src + 32, q : q + nq] = (mine + backs[n][...].astype(F32)).astype(BF)

    lanes = pl.ds(pl.multiple_of(y * SLICE, SLICE), SLICE)
    y_backs = []
    for k in (1, 3, 2):
        yp = lax.rem(y + k, RING)
        copy = pltpu.make_async_remote_copy(
            src_ref=frame.at[pl.ds(pl.multiple_of(LEFT + FUN * yp, 8), FUN)],
            dst_ref=y_out.at[:, :, :, lanes],
            send_sem=by_send.at[k - 1],
            recv_sem=by_recv.at[y],
            device_id=dev(base + yp),
            device_id_type=MESH,
        )
        copy.start()
        y_backs.append(copy)
    home = pltpu.make_async_copy(frame.at[my_rows], y_out.at[:, :, :, lanes], by_recv.at[y])
    home.start()

    for copy in started:
        copy.wait_send()
    for copy in v_copies:
        copy.wait()
    for copy in s_copies:
        copy.wait_send()
    for copy in own_rows:
        copy.wait_send()

    @pl.when(y <= 2)
    def _():
        for yp in range(RING):
            pltpu.make_async_copy(rows_out.at[0], rows_out.at[0], c_send.at[3 + yp]).wait()

    @pl.when(y >= 1)
    def _():
        for yp in range(RING):
            pltpu.make_async_copy(rows_out.at[2], rows_out.at[2], c_send.at[7 + yp]).wait()

    for copy in x_backs:
        copy.wait_send()
    for copy in y_backs:
        copy.wait_send()
    for ys in range(RING):
        part = y_out.at[:, :, :, pl.ds(ys * SLICE, SLICE)]
        pltpu.make_async_copy(part, part, by_recv.at[ys]).wait()


def filter_kernel(starts, pieces, kinetic, pot, out, pot_rows):
    step = pl.program_id(0)

    @pl.when(step == 0)
    def _():
        for k in range(7):
            pot_rows[BOX * k : BOX * k + BOX, :] = pot[k].astype(F32)[0:BOX]

    held = pieces[...]
    applied = jnp.dot(held, kinetic[...], preferred_element_type=F32)
    for j in range(8):
        rows = slice(SUP * j, SUP * j + SUP)
        start = starts[8 * step + j]
        rest = lax.rem(start, 8)
        local = pot_rows[pl.ds(pl.multiple_of(start - rest, 8), SUP + 8), :]
        local = pltpu.roll(local, lax.rem(SUP + 8 - rest, SUP + 8), 0)[0:SUP]
        out[rows, :] = (applied[rows] + local * held[rows].astype(F32)).astype(BF)


def on_device(coeffs, centers, kinetic, potential):
    me = lax.axis_index("func") * 16 + lax.axis_index("box")
    ring = me // RING
    around = jnp.concatenate([centers[-LEFT:], centers, centers[: FRAME - LEFT]])
    near = lax.dynamic_slice_in_dim(around, ring * OWN, FRAME)
    first = near[LEFT]
    rel = (near - first + OWN) % BOX_ALL
    octets = rel.reshape(32, 8)
    eight = jnp.arange(8, dtype=jnp.int32)
    steps = jnp.arange(SUP, dtype=jnp.int32)
    into = ((octets[:, :, None] + steps[None, None, :]) % SUP) * 8 + eight[None, :, None]
    outof = eight[None, None, :] * SUP + (steps[None, :, None] - octets[:, None, :]) % SUP
    low = jnp.broadcast_to(rel[LEFT] + 16, (1, FRAME))
    top = jnp.broadcast_to(rel[LEFT + OWN - 1] + 16, (1, FRAME))
    meta = jnp.concatenate(
        [
            rel.reshape(1, FRAME),
            low,
            top,
            jnp.zeros((5, FRAME), jnp.int32),
            into.reshape(32, FRAME),
            outof.reshape(32, FRAME),
        ]
    )
    my_centers = lax.dynamic_slice_in_dim(centers, me * FUN, FUN)
    starts = (my_centers - BOX * (me - 2)) % BOX_ALL

    hbm = pl.BlockSpec(memory_space=pl.ANY)
    vmem = pl.BlockSpec(memory_space=pltpu.VMEM)
    dma = pltpu.SemaphoreType.DMA
    pieces, pot, gram_band = pl.pallas_call(
        exchange_kernel,
        out_shape=(
            jax.ShapeDtypeStruct((FUN, 4, 8, 1024), BF),
            jax.ShapeDtypeStruct((7, 16, 1024), BF),
            jax.ShapeDtypeStruct((FUN, FRAME), F32),
        ),
        in_specs=[hbm, vmem, vmem],
        out_specs=(hbm, hbm, vmem),
        scratch_shapes=[
            pltpu.VMEM((FRAME, 4, 8, SLICE), BF),
            pltpu.VMEM((SUP, FRAME, SLICE), BF),
            pltpu.VMEM((32, 2, 8, SLICE), BF),
            pltpu.VMEM((32, 2, 8, SLICE), BF),
            pltpu.VMEM((32, 1, 8, SLICE), BF),
            pltpu.VMEM((32, 1, 8, SLICE), BF),
            pltpu.VMEM((FRAME, FRAME), F32),
            pltpu.VMEM((12, FUN, FRAME), F32),
            pltpu.VMEM((3, FUN, FRAME), F32),
            pltpu.VMEM((3, FUN, FRAME), BF),
            pltpu.VMEM((12, FUN, FRAME), BF),
            pltpu.VMEM((FRAME, FRAME), F32),
            pltpu.VMEM((16, 1024), BF),
            pltpu.VMEM((FRAME, FRAME), jnp.int32),
            dma((3, 4)), dma((4, 4)), dma((4,)), dma((4,)), dma((7,)), dma((7,)),
            dma((9,)), dma((12,)), dma((11,)), dma((12,)), dma((4,)), dma((4,)), dma((3,)), dma((4,)),
        ],
        compiler_params=pltpu.CompilerParams(collective_id=0, has_side_effects=True),
        name="exchange",
    )(coeffs.reshape(FUN, 4, 8, 1024), potential, meta)

    filtered = pl.pallas_call(
        filter_kernel,
        grid_spec=pltpu.PrefetchScalarGridSpec(
            num_scalar_prefetch=1,
            grid=(3,),
            in_specs=[
                pl.BlockSpec((256, 1024), lambda i, s: (i, 0)),
                pl.BlockSpec((1024, 1024), lambda i, s: (0, 0)),
                pl.BlockSpec((7, 16, 1024), lambda i, s: (0, 0, 0)),
            ],
            out_specs=pl.BlockSpec((256, 1024), lambda i, s: (i, 0)),
            scratch_shapes=[pltpu.VMEM((128, 1024), F32)],
        ),
        out_shape=jax.ShapeDtypeStruct((FUN * SUP, 1024), BF),
        name="filter",
    )(starts, pieces.reshape(FUN * SUP, 1024), kinetic, pot)
    return filtered.reshape(FUN, SUP, 1024), gram_band


def solution(mesh):
    placed = (P(("func", "box"), None, None), P(), P(), P(("func", "box"), None))
    return jax.shard_map(
        on_device,
        mesh=mesh,
        in_specs=placed,
        out_specs=(P(("func", "box"), None, None), P(("func", "box"), None)),
        check_vma=False,
    )
```

profile of v0, /device:TPU:0, one launch (start us, length us, event | category | flops | bytes accessed | tf_op | source)
XLA Modules:
  0.0 105.2 jit_solution(12447689619907298613)
XLA Ops:
  0.7 1.3 %and_select_fusion.1.starts = s32[24]{0:T(128)} fusion(s32[3072]{0:T(1024)} %param.5, s32[]{:T(128)S(6)} %select_n.37, s32[]{:T(128)S(6)} %mul_shard_map.3), kind=kLoop, calls=%fused_computation.13 | loop fusion | flops 168 | bytes 200 | tf_op jit(solution)/shard_map/jit(remainder)/select_n | solution.py:422
  2.0 0.8 slice.15
  2.7 0.7 slice.16
  3.4 0.1 add.123
  3.5 0.1 add.118
  3.6 0.8 concatenate.6
  4.4 0.1 dynamic_slice.7
  4.4 0.6 slice.17
  5.0 0.7 and_select_fusion
  5.8 0.6 fusion.5
  7.7 0.1 add.127
  7.8 0.1 add.114
  7.8 0.1 copy.6
  7.9 0.1 sub.46
  8.0 0.1 add.115
  8.1 0.1 add.116
  8.2 0.1 copy.7
  8.4 1.8 %concatenate.7.meta = s32[72,256]{1,0:T(8,128)} concatenate(s32[1,256]{1,0:T(1,128)S(1)} %bitcast.12, s32[1,256]{1,0:T(1,128)S(1)} %broadcast_in_dim.6, s32[1,256]{1,0:T(1,128)S(1)} %broadcast_in_dim.14, s32[5,256]{1,0:T(8,128)S(1)} %broadcast_in_dim.15, s32[32,256]{1,0:T(8,128)S(1)} %get-tuple-element.10, s32[32,256]{1,0:T(8,128)S(1)} %get-tuple-element.11), dimensions={0} | concatenate | bytes 147456 | tf_op jit(solution)/shard_map/concatenate | solution.py:411
  10.2 88.0 %exchange.1 = (bf16[24,4,8,1024]{3,2,1,0:T(8,128)(2,1)}, bf16[7,16,1024]{2,1,0:T(8,128)(2,1)}, f32[24,256]{1,0:T(8,128)}) custom-call(bf16[24,4,8,1024]{3,2,1,0:T(8,128)(2,1)} %bitcast.9, f32[12,1024]{1,0:T(8,128)} %pot.1, s32[72,256]{1,0:T(8,128)} %concatenate.7.meta), custom_call_target="tpu_custom_call" | custom-call | tf_op jit(solution)/shard_map/exchange/pallas_call | solution.py:427
  98.2 0.0 copy-start
  98.2 6.3 %filter.1 = bf16[768,1024]{1,0:T(8,128)(2,1)} custom-call(s32[24]{0:T(128)} %and_select_fusion.1.starts, bf16[768,1024]{1,0:T(8,128)(2,1)} %bitcast.11, bf16[1024,1024]{1,0:T(8,128)(2,1)} %kinetic.1, bf16[7,16,1024]{2,1,0:T(8,128)(2,1)} %get-tuple-element.6.pot), custom_call_target="tpu_custom_call" | custom-call | tf_op jit(solution)/shard_map/filter/pallas_call | solution.py:458
  104.5 0.0 copy-done
  104.5 0.6 copy.9
  (10 shorter events, 0.1 us)
Async XLA Ops:
  98.2 6.3 %copy-start = (f32[24,256]{1,0:T(8,128)S(1)}, f32[24,256]{1,0:T(8,128)}, u32[]{:S(2)}) copy-start(f32[24,256]{1,0:T(8,128)} %get-tuple-element.15) | copy-start | bytes 73732
where the time goes:
time: 107 us; the launch traced here: 105 us
  Pallas kernels  94.3 us (88%)
  local copies, waits for them, and re-layouts  6.76 us (6%)
  other arithmetic  2.08 us (2%)
  between operations  2 us (2%)
    pallas_call x1, Pallas kernels, on_device(): pl.pallas_call(exchange_kernel, out_shape=(jax.ShapeDtypeStruct((FUN, 4,...  88 us
    pallas_call x1, Pallas kernels, on_device(): pl.pallas_call(filter_kernel, grid_spec=pltpu.PrefetchScalarGridSpec(num_...  6.32 us

commit v1 on v0

--- a/solution.py
+++ b/solution.py
@@ -37,9 +37,11 @@
 
 
 def exchange_kernel(
-    coeffs, pot, meta, y_out, v_out, gram_out,
+    coeffs, kinetic, pot, lanes_in, out, gram_out,
     frame, slots, back_a, back_b, back_c, back_d, gram, terms, sums, rows_out, rows_in, mixing, potb, boxes,
-    y_send, y_recv, x_send, x_recv, v_send, v_recv, s_send, s_recv, c_send, c_recv, bx_send, bx_recv, by_send, by_recv,
+    meta, starts, kin, v_win, pot_rows, pot_own, y_in, x_in, y_res,
+    y_send, y_recv, x_send, x_recv, v_send, v_recv, s_send, s_recv, c_send, c_recv, bx_send, bx_recv,
+    by_send, by_recv, kin_sem, out_sem,
 ):
     me = lax.axis_index("func") * 16 + lax.axis_index("box")
     y = lax.rem(me, RING)
@@ -53,6 +55,9 @@
     for k in range(1, REACH + 1):
         for sign in (1, -1):
             pl.semaphore_signal(barrier, inc=1, device_id=dev(me + sign * k), device_id_type=MESH)
+
+    kin_copy = pltpu.make_async_copy(kinetic, kin, kin_sem)
+    kin_copy.start()
 
     frame[16:48, 0:3] = jnp.zeros((32, 3, 8, SLICE), BF)
     frame[48:80, 0:2] = jnp.zeros((32, 2, 8, SLICE), BF)
@@ -92,11 +97,11 @@
     v_copies = []
     for o in range(-2, 5):
         if o == 0:
-            copy = pltpu.make_async_copy(potb, v_out.at[2], v_recv.at[2])
+            copy = pltpu.make_async_copy(potb, v_win.at[2], v_recv.at[2])
         else:
             copy = pltpu.make_async_remote_copy(
                 src_ref=potb,
-                dst_ref=v_out.at[o + 2],
+                dst_ref=v_win.at[o + 2],
                 send_sem=v_send.at[o + 2],
                 recv_sem=v_recv.at[o + 2],
                 device_id=dev(me - o),
@@ -104,6 +109,55 @@
             )
         copy.start()
         v_copies.append(copy)
+
+    ring = lax.div(me, RING)
+    flat = ring * OWN - LEFT + FUN_ALL
+    top_line = lax.div(flat, 128)
+    lines = [lanes_in[pl.ds(lax.rem(top_line + k, FUN_ALL // 128), 1), :] for k in range(3)]
+    near = pltpu.roll(jnp.concatenate(lines, axis=1), 384 - lax.rem(flat, 128), 1)[:, 0:FRAME]
+    row_lane = lax.broadcasted_iota(jnp.int32, (1, FRAME), 1)
+
+    def pick(row, lane_at):
+        return jnp.sum(jnp.where(row_lane == lane_at, row, 0), axis=1, keepdims=True)
+
+    rel_row = near - pick(near, LEFT) + OWN
+    rel_row = jnp.where(rel_row < 0, rel_row + BOX_ALL, rel_row)
+    rel_row = jnp.where(rel_row >= BOX_ALL, rel_row - BOX_ALL, rel_row)
+    low_row = OWN + 16
+    top_row = pick(rel_row, LEFT + OWN - 1) + 16
+    row_id = lax.broadcasted_iota(jnp.int32, (FRAME, FRAME), 0)
+    col_id = lax.broadcasted_iota(jnp.int32, (FRAME, FRAME), 1)
+    rel_tile = jnp.broadcast_to(rel_row, (FRAME, FRAME))
+    rel_col = jnp.sum(
+        jnp.where(row_id == col_id, rel_tile.astype(F32), 0.0), axis=1, keepdims=True
+    ).astype(jnp.int32)
+    boxes[...] = jnp.broadcast_to(rel_col, (FRAME, 128))
+    sub_o = lax.broadcasted_iota(jnp.int32, (32, FRAME), 0)
+    lane_o = lax.broadcasted_iota(jnp.int32, (32, FRAME), 1)
+    rest_row = jnp.bitwise_and(rel_row, SUP - 1)
+    spread = jnp.where(
+        lax.shift_right_logical(lane_o, 3) == sub_o, jnp.broadcast_to(rest_row, (32, FRAME)), 0
+    ).astype(F32).astype(BF)
+    in_octet = jnp.bitwise_and(row_id, 7)
+    by_fun = (in_octet == lax.shift_right_logical(col_id, 5)).astype(F32).astype(BF)
+    by_low = (in_octet == jnp.bitwise_and(col_id, 7)).astype(F32).astype(BF)
+    rest_fun = jnp.dot(spread, by_fun, preferred_element_type=F32).astype(jnp.int32)
+    rest_low = jnp.dot(spread, by_low, preferred_element_type=F32).astype(jnp.int32)
+    meta[0:32, :] = jnp.bitwise_and(rest_fun + lane_o, SUP - 1) * 8 + lax.shift_right_logical(lane_o, 5)
+    meta[32:64, :] = jnp.bitwise_and(lane_o, 7) * SUP + jnp.bitwise_and(
+        lax.shift_right_logical(lane_o, 3) - rest_low, SUP - 1
+    )
+
+    start_row = near - BOX * (me - 2)
+    start_row = jnp.where(start_row < 0, start_row + BOX_ALL, start_row)
+    start_row = jnp.where(start_row >= BOX_ALL, start_row - BOX_ALL, start_row)
+    start_row = jnp.minimum(start_row, 127)
+    spread = jnp.where(
+        lax.shift_right_logical(lane_o, 3) == sub_o, jnp.broadcast_to(start_row, (32, FRAME)), 0
+    ).astype(F32).astype(BF)
+    starts[...] = jnp.dot(spread, by_fun, preferred_element_type=F32).astype(jnp.int32) + jnp.bitwise_and(
+        lane_o, SUP - 1
+    )
 
     arrived = set()
 
@@ -132,14 +186,11 @@
         for q in range(4):
             wait_piece(ys, q)
 
-    row_id = lax.broadcasted_iota(jnp.int32, (FRAME, FRAME), 0)
-    col_id = lax.broadcasted_iota(jnp.int32, (FRAME, FRAME), 1)
-
     def into_slots(pair, carry):
         parts = []
         for half in range(2):
             octet = 2 * pair + half
-            select = (row_id == meta[pl.ds(8 + octet, 1), :]).astype(F32).astype(BF)
+            select = (row_id == meta[pl.ds(octet, 1), :]).astype(F32).astype(BF)
             raw = frame[pl.ds(pl.multiple_of(8 * octet, 8), 8)]
             raw = raw.astype(F32).reshape(FRAME, SLICE).astype(BF)
             out = jnp.dot(select, raw, preferred_element_type=F32)
@@ -154,32 +205,30 @@
     lax.fori_loop(1, 5, into_slots, 0)
     lax.fori_loop(11, 15, into_slots, 0)
 
-    rel_row = meta[0:1, :]
-    rel_tile = jnp.broadcast_to(rel_row, (FRAME, FRAME))
-    rel_col = jnp.sum(
-        jnp.where(row_id == col_id, rel_tile.astype(F32), 0.0), axis=1, keepdims=True
-    ).astype(jnp.int32)
-    low_row = meta[1:2, :]
-    top_row = meta[2:3, :]
-    boxes[...] = jnp.broadcast_to(rel_col, (FRAME, FRAME))
-
     def same_box(slot):
         box_row = rel_row + jnp.bitwise_and(slot - rel_row, SUP - 1)
         owned = jnp.logical_and(box_row >= low_row, box_row <= top_row)
         box_row = jnp.where(owned, box_row, -1)
         col = boxes[...]
         box_col = col + jnp.bitwise_and(slot - col, SUP - 1)
-        return box_col == box_row
+        return box_col == box_row[:, 0:128], box_col == box_row[:, 128:256]
 
     gram[...] = jnp.zeros((FRAME, FRAME), F32)
 
-    def gram_step(slot, carry):
-        held = slots[slot]
-        prod = lax.dot_general(held, held, (((1,), (1,)), ((), ())), preferred_element_type=F32)
-        gram[...] += jnp.where(same_box(slot), prod, 0.0)
+    def gram_step(step, carry):
+        lo, hi = gram[:, 0:128], gram[:, 128:256]
+        for part in range(4):
+            slot = 4 * step + part
+            held = slots[slot]
+            prod = lax.dot_general(held, held, (((1,), (1,)), ((), ())), preferred_element_type=F32)
+            same_lo, same_hi = same_box(slot)
+            lo = lo + jnp.where(same_lo, prod[:, 0:128], 0.0)
+            hi = hi + jnp.where(same_hi, prod[:, 128:256], 0.0)
+        gram[:, 0:128] = lo
+        gram[:, 128:256] = hi
         return carry
 
-    lax.fori_loop(0, SUP, gram_step, 0)
+    lax.fori_loop(0, SUP // 4, gram_step, 0)
     gram[...] = gram[...] * VOLUME
 
     s_copies = []
@@ -203,6 +252,22 @@
         send_terms(2 + yp, FUN * yp - 16, 8 + y, base - RING + yp)
     for yp in range(0, 3):
         send_terms(6 + yp, 176 + FUN * yp, y, base + RING + yp)
+
+    for copy in v_copies:
+        if copy is v_copies[2]:
+            copy.wait()
+        else:
+            copy.wait_recv()
+    for k in range(7):
+        pot_rows[BOX * k : BOX * k + BOX, :] = v_win[k].astype(F32)[0:BOX]
+    pot_rows[7 * BOX : 128, :] = jnp.zeros((128 - 7 * BOX, 1024), F32)
+
+    near_rows = pot_rows[...].astype(BF)
+    row_of = lax.broadcasted_iota(jnp.int32, (128, FRAME), 0)
+    for j in range(3):
+        select = (row_of == starts[pl.ds(LEFT // 8 + 3 * y + j, 1), :]).astype(F32).astype(BF)
+        local = lax.dot_general(select, near_rows, (((0,), (0,)), ((), ())), preferred_element_type=F32)
+        pot_own[8 * j : 8 * j + 8] = local.reshape(8, 4, 8, 1024)
 
     def wait_terms(slot):
         pltpu.make_async_copy(terms.at[slot], terms.at[slot], s_recv.at[slot]).wait()
@@ -289,12 +354,17 @@
         wait_rows(ys)
         mixing[FUN * ys - 16 : FUN * ys + 8, :] = rows_in[ys].astype(F32)
 
-    def mix_step(slot, carry):
-        mix = jnp.where(same_box(slot), mixing[...], 0.0).astype(BF)
-        slots[slot] = jnp.dot(mix, slots[slot], preferred_element_type=F32).astype(BF)
+    def mix_step(step, carry):
+        for part in range(4):
+            slot = 4 * step + part
+            same_lo, same_hi = same_box(slot)
+            mix = jnp.concatenate(
+                [jnp.where(same_lo, mixing[:, 0:128], 0.0), jnp.where(same_hi, mixing[:, 128:256], 0.0)], axis=1
+            ).astype(BF)
+            slots[slot] = jnp.dot(mix, slots[slot], preferred_element_type=F32).astype(BF)
         return carry
 
-    lax.fori_loop(0, SUP, mix_step, 0)
+    lax.fori_loop(0, SUP // 4, mix_step, 0)
 
     for copy in forwards:
         copy.wait_send()
@@ -303,7 +373,7 @@
         both = slots[:, pl.ds(pl.multiple_of(16 * pair, 16), 16), :].astype(F32)
         for half in range(2):
             octet = 2 * pair + half
-            select = (row_id == meta[pl.ds(40 + octet, 1), :]).astype(F32).astype(BF)
+            select = (row_id == meta[pl.ds(32 + octet, 1), :]).astype(F32).astype(BF)
             part = both[:, 8 * half : 8 * half + 8, :].reshape(FRAME, SLICE).astype(BF)
             out = jnp.dot(select, part, preferred_element_type=F32)
             frame[pl.ds(pl.multiple_of(8 * octet, 8), 8)] = out.reshape(8, 4, 8, SLICE).astype(BF)
@@ -325,32 +395,85 @@
         copy.start()
         x_backs.append(copy)
     lax.fori_loop(5, 11, out_of_slots, 0)
+
+    lanes = pl.ds(pl.multiple_of(y * SLICE, SLICE), SLICE)
+    y_backs = []
+
+    def quarters(octet):
+        unit = lax.div(octet, 4)
+        clean = 2 - unit
+        first = 2 * lax.div(unit, 2)
+        second = 3 - 2 * lax.div(3 - unit, 3)
+        return ((clean, 2),), ((first, 1), (second, 1))
+
+    def send_home(which):
+        for k in (1, 3, 2, 0):
+            yp = lax.rem(y + k, RING)
+            for j in range(3):
+                for n, (q, nq) in enumerate(quarters(3 * yp + j)[which]):
+                    src = frame.at[pl.ds(pl.multiple_of(LEFT + FUN * yp + 8 * j, 8), 8), pl.ds(q, nq)]
+                    dst = y_in.at[pl.ds(8 * j, 8), pl.ds(q, nq), :, lanes]
+                    if k == 0:
+                        pltpu.make_async_copy(src, dst, by_recv.at[y, j, which + n]).start()
+                        continue
+                    copy = pltpu.make_async_remote_copy(
+                        src_ref=src,
+                        dst_ref=dst,
+                        send_sem=by_send.at[k - 1, j, which + n],
+                        recv_sem=by_recv.at[y, j, which + n],
+                        device_id=dev(base + yp),
+                        device_id_type=MESH,
+                    )
+                    copy.start()
+                    y_backs.append(copy)
+
+    send_home(0)
     for n, (src, q, nq, dst, to) in enumerate(FORWARD):
         x_backs[n].wait_recv()
         mine = frame[src : src + 32, q : q + nq].astype(F32)
         frame[src : src + 32, q : q + nq] = (mine + backs[n][...].astype(F32)).astype(BF)
-
-    lanes = pl.ds(pl.multiple_of(y * SLICE, SLICE), SLICE)
-    y_backs = []
-    for k in (1, 3, 2):
-        yp = lax.rem(y + k, RING)
-        copy = pltpu.make_async_remote_copy(
-            src_ref=frame.at[pl.ds(pl.multiple_of(LEFT + FUN * yp, 8), FUN)],
-            dst_ref=y_out.at[:, :, :, lanes],
-            send_sem=by_send.at[k - 1],
-            recv_sem=by_recv.at[y],
-            device_id=dev(base + yp),
-            device_id_type=MESH,
-        )
-        copy.start()
-        y_backs.append(copy)
-    home = pltpu.make_async_copy(frame.at[my_rows], y_out.at[:, :, :, lanes], by_recv.at[y])
-    home.start()
+    send_home(1)
+
+    kin_copy.wait()
+    out_copies = []
+    for which in range(2):
+        for j in range(3):
+            octs = quarters(3 * y + j)[which]
+            for n, (q, nq) in enumerate(octs):
+                for ys in range(RING):
+                    part = y_in.at[pl.ds(8 * j, 8), pl.ds(q, nq), :, pl.ds(ys * SLICE, SLICE)]
+                    pltpu.make_async_copy(part, part, by_recv.at[ys, j, which + n]).wait()
+                rows = 8 * 8 * nq
+                at = 128 * j + rows * n
+                piece = y_in[8 * j : 8 * j + 8, pl.ds(q, nq)].astype(F32).reshape(rows, 1024)
+                x_in[at : at + rows, :] = piece.astype(BF)
+        for t in range(4):
+            cols = slice(256 * t, 256 * t + 256)
+            applied = jnp.dot(x_in[...], kin[:, cols], preferred_element_type=F32)
+            for j in range(3):
+                octs = quarters(3 * y + j)[which]
+                for n, (q, nq) in enumerate(octs):
+                    rows = 8 * 8 * nq
+                    at = 128 * j + rows * n
+                    local = pot_own[8 * j : 8 * j + 8, pl.ds(q, nq), :, cols].reshape(rows, 256)
+                    res = applied[at : at + rows] + local * x_in[at : at + rows, cols].astype(F32)
+                    y_res[8 * j : 8 * j + 8, pl.ds(q, nq), :, cols] = res.reshape(8, nq, 8, 256).astype(BF)
+        for j in range(3):
+            octs = quarters(3 * y + j)[which]
+            for n, (q, nq) in enumerate(octs):
+                copy = pltpu.make_async_copy(
+                    y_res.at[pl.ds(8 * j, 8), pl.ds(q, nq)],
+                    out.at[pl.ds(8 * j, 8), pl.ds(q, nq)],
+                    out_sem.at[j, which + n],
+                )
+                copy.start()
+                out_copies.append(copy)
 
     for copy in started:
         copy.wait_send()
-    for copy in v_copies:
-        copy.wait()
+    for k, copy in enumerate(v_copies):
+        if k != 2:
+            copy.wait_send()
     for copy in s_copies:
         copy.wait_send()
     for copy in own_rows:
@@ -370,69 +493,22 @@
         copy.wait_send()
     for copy in y_backs:
         copy.wait_send()
-    for ys in range(RING):
-        part = y_out.at[:, :, :, pl.ds(ys * SLICE, SLICE)]
-        pltpu.make_async_copy(part, part, by_recv.at[ys]).wait()
-
-
-def filter_kernel(starts, pieces, kinetic, pot, out, pot_rows):
-    step = pl.program_id(0)
-
-    @pl.when(step == 0)
-    def _():
-        for k in range(7):
-            pot_rows[BOX * k : BOX * k + BOX, :] = pot[k].astype(F32)[0:BOX]
-
-    held = pieces[...]
-    applied = jnp.dot(held, kinetic[...], preferred_element_type=F32)
-    for j in range(8):
-        rows = slice(SUP * j, SUP * j + SUP)
-        start = starts[8 * step + j]
-        rest = lax.rem(start, 8)
-        local = pot_rows[pl.ds(pl.multiple_of(start - rest, 8), SUP + 8), :]
-        local = pltpu.roll(local, lax.rem(SUP + 8 - rest, SUP + 8), 0)[0:SUP]
-        out[rows, :] = (applied[rows] + local * held[rows].astype(F32)).astype(BF)
+    for copy in out_copies:
+        copy.wait()
 
 
 def on_device(coeffs, centers, kinetic, potential):
-    me = lax.axis_index("func") * 16 + lax.axis_index("box")
-    ring = me // RING
-    around = jnp.concatenate([centers[-LEFT:], centers, centers[: FRAME - LEFT]])
-    near = lax.dynamic_slice_in_dim(around, ring * OWN, FRAME)
-    first = near[LEFT]
-    rel = (near - first + OWN) % BOX_ALL
-    octets = rel.reshape(32, 8)
-    eight = jnp.arange(8, dtype=jnp.int32)
-    steps = jnp.arange(SUP, dtype=jnp.int32)
-    into = ((octets[:, :, None] + steps[None, None, :]) % SUP) * 8 + eight[None, :, None]
-    outof = eight[None, None, :] * SUP + (steps[None, :, None] - octets[:, None, :]) % SUP
-    low = jnp.broadcast_to(rel[LEFT] + 16, (1, FRAME))
-    top = jnp.broadcast_to(rel[LEFT + OWN - 1] + 16, (1, FRAME))
-    meta = jnp.concatenate(
-        [
-            rel.reshape(1, FRAME),
-            low,
-            top,
-            jnp.zeros((5, FRAME), jnp.int32),
-            into.reshape(32, FRAME),
-            outof.reshape(32, FRAME),
-        ]
-    )
-    my_centers = lax.dynamic_slice_in_dim(centers, me * FUN, FUN)
-    starts = (my_centers - BOX * (me - 2)) % BOX_ALL
-
     hbm = pl.BlockSpec(memory_space=pl.ANY)
     vmem = pl.BlockSpec(memory_space=pltpu.VMEM)
     dma = pltpu.SemaphoreType.DMA
-    pieces, pot, gram_band = pl.pallas_call(
+    filtered, gram_band = pl.pallas_call(
         exchange_kernel,
         out_shape=(
             jax.ShapeDtypeStruct((FUN, 4, 8, 1024), BF),
-            jax.ShapeDtypeStruct((7, 16, 1024), BF),
             jax.ShapeDtypeStruct((FUN, FRAME), F32),
         ),
-        in_specs=[hbm, vmem, vmem],
-        out_specs=(hbm, hbm, vmem),
+        in_specs=[hbm, hbm, vmem, vmem],
+        out_specs=(hbm, vmem),
         scratch_shapes=[
             pltpu.VMEM((FRAME, 4, 8, SLICE), BF),
             pltpu.VMEM((SUP, FRAME, SLICE), BF),
@@ -447,30 +523,23 @@
             pltpu.VMEM((12, FUN, FRAME), BF),
             pltpu.VMEM((FRAME, FRAME), F32),
             pltpu.VMEM((16, 1024), BF),
-            pltpu.VMEM((FRAME, FRAME), jnp.int32),
+            pltpu.VMEM((FRAME, 128), jnp.int32),
+            pltpu.VMEM((64, FRAME), jnp.int32),
+            pltpu.VMEM((32, FRAME), jnp.int32),
+            pltpu.VMEM((1024, 1024), BF),
+            pltpu.VMEM((7, 16, 1024), BF),
+            pltpu.VMEM((128, 1024), F32),
+            pltpu.VMEM((FUN, 4, 8, 1024), F32),
+            pltpu.VMEM((FUN, 4, 8, 1024), BF),
+            pltpu.VMEM((384, 1024), BF),
+            pltpu.VMEM((FUN, 4, 8, 1024), BF),
             dma((3, 4)), dma((4, 4)), dma((4,)), dma((4,)), dma((7,)), dma((7,)),
-            dma((9,)), dma((12,)), dma((11,)), dma((12,)), dma((4,)), dma((4,)), dma((3,)), dma((4,)),
+            dma((9,)), dma((12,)), dma((11,)), dma((12,)), dma((4,)), dma((4,)),
+            dma((3, 3, 3)), dma((4, 3, 3)), dma, dma((3, 3)),
         ],
         compiler_params=pltpu.CompilerParams(collective_id=0, has_side_effects=True),
         name="exchange",
-    )(coeffs.reshape(FUN, 4, 8, 1024), potential, meta)
-
-    filtered = pl.pallas_call(
-        filter_kernel,
-        grid_spec=pltpu.PrefetchScalarGridSpec(
-            num_scalar_prefetch=1,
-            grid=(3,),
-            in_specs=[
-                pl.BlockSpec((256, 1024), lambda i, s: (i, 0)),
-                pl.BlockSpec((1024, 1024), lambda i, s: (0, 0)),
-                pl.BlockSpec((7, 16, 1024), lambda i, s: (0, 0, 0)),
-            ],
-            out_specs=pl.BlockSpec((256, 1024), lambda i, s: (i, 0)),
-            scratch_shapes=[pltpu.VMEM((128, 1024), F32)],
-        ),
-        out_shape=jax.ShapeDtypeStruct((FUN * SUP, 1024), BF),
-        name="filter",
-    )(starts, pieces.reshape(FUN * SUP, 1024), kinetic, pot)
+    )(coeffs.reshape(FUN, 4, 8, 1024), kinetic, potential, centers.reshape(FUN, 128))
     return filtered.reshape(FUN, SUP, 1024), gram_band
 
 

time: 107 us -> 79.1 us (0.74); the launches traced: 105 us -> 78.9 us
  Pallas kernels: 94.3 us -> 74.9 us
  local copies, waits for them, and re-layouts: 6.76 us -> 3.36 us
  other arithmetic: 2.08 us -> 0 us
  between operations: 2 us -> 0.65 us
    pallas_call x1, Pallas kernels: 88 us -> 74.9 us  [on_device(): pl.pallas_call(exchange_kernel, out_shape=(jax.ShapeDtypeStruct((FUN, 4,...]
    pallas_call x1 -> x0, Pallas kernels: 6.32 us -> none  [on_device(): pl.pallas_call(filter_kernel, grid_spec=pltpu.PrefetchScalarGridSpec(num_...]
    unnamed x3 -> x4, local copies, waits for them, and re-layouts: 0.61 us -> 3.36 us
    slice x4 -> x0, local copies, waits for them, and re-layouts: 2.65 us -> none  [the longest x2 1.44 us: on_device(): around = jnp.concatenate([centers[-LEFT:], centers, centers[:FRAME - LEFT]])]
    concatenate x2 -> x0, local copies, waits for them, and re-layouts: 2.63 us -> none  [the longest x1 1.85 us: on_device(): jnp.concatenate([rel.reshape(1, FRAME), low, top, jnp.zeros((5, FRAME), j...]
    select_n x2 -> x0, other arithmetic: 2.03 us -> none  [the longest x1 1.3 us: on_device(): starts = (my_centers - BOX * (me - 2)) % BOX_ALL]
where the time goes in v1:
time: 79.1 us; the launch traced here: 78.9 us
  Pallas kernels  74.9 us (95%)
  local copies, waits for them, and re-layouts  3.36 us (4%)
    pallas_call x1, Pallas kernels, on_device(): pl.pallas_call(exchange_kernel, out_shape=(jax.ShapeDtypeStruct((FUN, 4,...  74.9 us
    unnamed x4, local copies, waits for them, and re-layouts  3.36 us

profile of v1, /device:TPU:0, one launch (start us, length us, event | category | flops | bytes accessed | tf_op | source)
XLA Modules:
  0.0 78.9 jit_solution(12103707070334749287)
XLA Ops:
  0.6 74.9 %exchange.1 = (bf16[24,4,8,1024]{3,2,1,0:T(8,128)(2,1)}, f32[24,256]{1,0:T(8,128)}) custom-call(bf16[24,4,8,1024]{3,2,1,0:T(8,128)(2,1)} %bitcast.3, bf16[1024,1024]{1,0:T(8,128)(2,1)} %kinetic.1, f32[12,1024]{1,0:T(8,128)} %pot.1, s32[24,128]{1,0:T(8,128)} %bitcast.5), custom_call_target="tpu_custom_call" | custom-call | tf_op jit(solution)/shard_map/exchange/pallas_call | solution.py:504
  75.5 0.0 copy-start
  75.5 2.7 %copy.8 = bf16[24,32,1024]{2,1,0:T(8,128)(2,1)} copy(bf16[24,32,1024]{2,1,0:T(8,128)(2,1)} %bitcast.4) | data formatting | bytes 3145728
  78.3 0.0 copy-done
  78.3 0.6 copy.9
Async XLA Ops:
  75.5 2.8 %copy-start = (f32[24,256]{1,0:T(8,128)S(1)}, f32[24,256]{1,0:T(8,128)}, u32[]{:S(2)}) copy-start(f32[24,256]{1,0:T(8,128)} %get-tuple-element.9) | copy-start | bytes 73732

commit v2 on v1

--- a/solution.py
+++ b/solution.py
@@ -17,28 +17,35 @@
 FRAME = 256
 LEFT = 80
 SLICE = 256
-REACH = 7
 BOX_ALL = 1536
 FUN_ALL = 3072
+W_HALO = 4
+W_OWN = 6
 VOLUME = 1.0 / (32 * 1024)
 
-FORWARD = (
+HALO = (
     (80, 0, 2, 176, -1),
     (144, 2, 2, 48, 1),
     (112, 0, 1, 208, -1),
     (112, 3, 1, 16, 1),
 )
-NEEDS = (
-    ((0, 0), (0, 1), (1, 0), (1, 1)),
-    ((3, 3), (3, 2), (2, 3), (2, 2)),
-    ((1, 0), (2, 0)),
-    ((2, 3), (1, 3)),
+FORWARD = (
+    (0, 0, 0, 24, -1),
+    (3, 3, 0, 24, 1),
+    (1, 0, 0, 24, -1),
+    (2, 3, 0, 24, 1),
+    (0, 1, 0, 24, -1),
+    (3, 2, 0, 24, 1),
+    (2, 0, 0, 16, -1),
+    (1, 3, 8, 16, 1),
+    (1, 1, 0, 8, -1),
+    (2, 2, 16, 8, 1),
 )
 
 
 def exchange_kernel(
     coeffs, kinetic, pot, lanes_in, out, gram_out,
-    frame, slots, back_a, back_b, back_c, back_d, gram, terms, sums, rows_out, rows_in, mixing, potb, boxes,
+    frame, slots, gram_out_rows, back_a, back_b, back_c, back_d, gram, terms, sums, rows_out, rows_in, mixing, potb, boxes,
     meta, starts, kin, v_win, pot_rows, pot_own, y_in, x_in, y_res,
     y_send, y_recv, x_send, x_recv, v_send, v_recv, s_send, s_recv, c_send, c_recv, bx_send, bx_recv,
     by_send, by_recv, kin_sem, out_sem,
@@ -52,9 +59,9 @@
         return (lax.div(wrapped, 16), lax.rem(wrapped, 16))
 
     barrier = pltpu.get_barrier_semaphore()
-    for k in range(1, REACH + 1):
-        for sign in (1, -1):
-            pl.semaphore_signal(barrier, inc=1, device_id=dev(me + sign * k), device_id_type=MESH)
+    partners = [base + lax.rem(y + k, RING) for k in range(1, RING)] + [me + RING, me - RING]
+    for partner in partners:
+        pl.semaphore_signal(barrier, inc=1, device_id=dev(partner), device_id_type=MESH)
 
     kin_copy = pltpu.make_async_copy(kinetic, kin, kin_sem)
     kin_copy.start()
@@ -67,14 +74,16 @@
     slots[:, 240:256, :] = jnp.zeros((SUP, 16, SLICE), BF)
     potb[0:BOX, :] = pot[...].astype(BF)
     potb[BOX:16, :] = jnp.zeros((16 - BOX, 1024), BF)
-    pl.semaphore_wait(barrier, 2 * REACH)
+    pl.semaphore_wait(barrier, len(partners))
 
     started = []
 
     my_rows = pl.ds(pl.multiple_of(LEFT + FUN * y, 8), FUN)
     high = lax.div(y, 2)
+    inner = lax.rem(lax.div(y + 1, 2), 2)
+
     for p in range(4):
-        q0 = (0, 1, 3, 2)[p]
+        q0 = p + inner * ((0, 3, 1, 2)[p] - p)
         q = q0 + high * (3 - 2 * q0)
         for k in (1, 3, 2):
             yp = lax.rem(y + k, RING)
@@ -93,22 +102,6 @@
             frame.at[my_rows, q],
             y_recv.at[y, q],
         ).start()
-
-    v_copies = []
-    for o in range(-2, 5):
-        if o == 0:
-            copy = pltpu.make_async_copy(potb, v_win.at[2], v_recv.at[2])
-        else:
-            copy = pltpu.make_async_remote_copy(
-                src_ref=potb,
-                dst_ref=v_win.at[o + 2],
-                send_sem=v_send.at[o + 2],
-                recv_sem=v_recv.at[o + 2],
-                device_id=dev(me - o),
-                device_id_type=MESH,
-            )
-        copy.start()
-        v_copies.append(copy)
 
     ring = lax.div(me, RING)
     flat = ring * OWN - LEFT + FUN_ALL
@@ -169,12 +162,12 @@
         pltpu.make_async_copy(piece, piece, y_recv.at[ys, q]).wait()
 
     forwards = []
-    for n, (src, q, nq, dst, to) in enumerate(FORWARD):
-        for ys, quarter in NEEDS[n]:
-            wait_piece(ys, quarter)
+    for n, (ys, q, first, count, to) in enumerate(FORWARD):
+        wait_piece(ys, q)
+        src = LEFT + FUN * ys + first
         copy = pltpu.make_async_remote_copy(
-            src_ref=frame.at[pl.ds(src, 32), pl.ds(q, nq)],
-            dst_ref=frame.at[pl.ds(dst, 32), pl.ds(q, nq)],
+            src_ref=frame.at[pl.ds(src, count), q],
+            dst_ref=frame.at[pl.ds(src - OWN * to, count), q],
             send_sem=x_send.at[n],
             recv_sem=x_recv.at[n],
             device_id=dev(me + RING * to),
@@ -182,9 +175,14 @@
         )
         copy.start()
         forwards.append(copy)
-    for ys in range(RING):
-        for q in range(4):
-            wait_piece(ys, q)
+
+    def pairs(step_of, first, count, width):
+        def several(step, carry):
+            for k in range(width):
+                step_of(first + width * step + k, carry)
+            return carry
+
+        lax.fori_loop(0, count // width, several, 0)
 
     def into_slots(pair, carry):
         parts = []
@@ -199,11 +197,31 @@
         slots[:, pl.ds(pl.multiple_of(16 * pair, 16), 16), :] = both
         return carry
 
-    lax.fori_loop(5, 11, into_slots, 0)
     for copy in forwards:
         copy.wait_recv()
-    lax.fori_loop(1, 5, into_slots, 0)
-    lax.fori_loop(11, 15, into_slots, 0)
+    pairs(into_slots, 1, 4, W_HALO)
+    pairs(into_slots, 11, 4, W_HALO)
+    for ys in range(RING):
+        for q in range(4):
+            wait_piece(ys, q)
+
+    v_copies = []
+    for o in range(-2, 5):
+        if o == 0:
+            copy = pltpu.make_async_copy(potb, v_win.at[2], v_recv.at[2])
+        else:
+            copy = pltpu.make_async_remote_copy(
+                src_ref=potb,
+                dst_ref=v_win.at[o + 2],
+                send_sem=v_send.at[o + 2],
+                recv_sem=v_recv.at[o + 2],
+                device_id=dev(me - o),
+                device_id_type=MESH,
+            )
+        copy.start()
+        v_copies.append(copy)
+
+    pairs(into_slots, 5, 6, W_OWN)
 
     def same_box(slot):
         box_row = rel_row + jnp.bitwise_and(slot - rel_row, SUP - 1)
@@ -229,13 +247,15 @@
         return carry
 
     lax.fori_loop(0, SUP // 4, gram_step, 0)
-    gram[...] = gram[...] * VOLUME
+    scaled = gram[...] * VOLUME
+    gram[...] = scaled
+    gram_out_rows[...] = scaled.reshape(FRAME // 8, 8, FRAME).astype(BF)
 
     s_copies = []
 
     def send_terms(n, start, slot, target):
         copy = pltpu.make_async_remote_copy(
-            src_ref=gram.at[pl.ds(start, FUN)],
+            src_ref=gram_out_rows.at[pl.ds(start, FUN // 8)],
             dst_ref=terms.at[slot],
             send_sem=s_send.at[n],
             recv_sem=s_recv.at[slot],
@@ -245,13 +265,13 @@
         copy.start()
         s_copies.append(copy)
 
+    for yp in range(1, 4):
+        send_terms(2 + yp, 3 * yp - 2, 8 + y, base - RING + yp)
+    for yp in range(0, 3):
+        send_terms(6 + yp, 22 + 3 * yp, y, base + RING + yp)
     for k in range(1, 4):
         yp = lax.rem(y + k, RING)
-        send_terms(k - 1, pl.multiple_of(LEFT + FUN * yp, 8), 4 + y, base + yp)
-    for yp in range(1, 4):
-        send_terms(2 + yp, FUN * yp - 16, 8 + y, base - RING + yp)
-    for yp in range(0, 3):
-        send_terms(6 + yp, 176 + FUN * yp, y, base + RING + yp)
+        send_terms(k - 1, LEFT // 8 + 3 * yp, 4 + y, base + yp)
 
     for copy in v_copies:
         if copy is v_copies[2]:
@@ -272,25 +292,28 @@
     def wait_terms(slot):
         pltpu.make_async_copy(terms.at[slot], terms.at[slot], s_recv.at[slot]).wait()
 
+    def arrived_terms(slot):
+        return terms[slot].astype(F32).reshape(FUN, FRAME)
+
     sums[0] = jnp.zeros((FUN, FRAME), F32)
     sums[2] = jnp.zeros((FUN, FRAME), F32)
     sums[1] = gram[my_rows, :]
     for k in range(1, 4):
         slot = 4 + lax.rem(y + k, RING)
         wait_terms(slot)
-        sums[1] += terms[slot]
+        sums[1] += arrived_terms(slot)
 
     @pl.when(y <= 2)
     def _():
         for ys in range(RING):
             wait_terms(ys)
-        sums[0] = terms[0] + terms[1] + terms[2] + terms[3]
+        sums[0] = arrived_terms(0) + arrived_terms(1) + arrived_terms(2) + arrived_terms(3)
 
     @pl.when(y >= 1)
     def _():
         for ys in range(RING):
             wait_terms(8 + ys)
-        sums[2] = terms[8] + terms[9] + terms[10] + terms[11]
+        sums[2] = arrived_terms(8) + arrived_terms(9) + arrived_terms(10) + arrived_terms(11)
 
     pad = jnp.zeros((FUN, FRAME), F32)
     wide = jnp.concatenate([sums[0], pad], axis=1)
@@ -379,11 +402,11 @@
             frame[pl.ds(pl.multiple_of(8 * octet, 8), 8)] = out.reshape(8, 4, 8, SLICE).astype(BF)
         return carry
 
-    lax.fori_loop(1, 5, out_of_slots, 0)
-    lax.fori_loop(11, 15, out_of_slots, 0)
+    pairs(out_of_slots, 1, 4, W_HALO)
+    pairs(out_of_slots, 11, 4, W_HALO)
     backs = (back_a, back_b, back_c, back_d)
     x_backs = []
-    for n, (src, q, nq, dst, to) in enumerate(FORWARD):
+    for n, (src, q, nq, dst, to) in enumerate(HALO):
         copy = pltpu.make_async_remote_copy(
             src_ref=frame.at[pl.ds(dst, 32), pl.ds(q, nq)],
             dst_ref=backs[n],
@@ -394,7 +417,7 @@
         )
         copy.start()
         x_backs.append(copy)
-    lax.fori_loop(5, 11, out_of_slots, 0)
+    pairs(out_of_slots, 5, 6, W_OWN)
 
     lanes = pl.ds(pl.multiple_of(y * SLICE, SLICE), SLICE)
     y_backs = []
@@ -428,7 +451,7 @@
                     y_backs.append(copy)
 
     send_home(0)
-    for n, (src, q, nq, dst, to) in enumerate(FORWARD):
+    for n, (src, q, nq, dst, to) in enumerate(HALO):
         x_backs[n].wait_recv()
         mine = frame[src : src + 32, q : q + nq].astype(F32)
         frame[src : src + 32, q : q + nq] = (mine + backs[n][...].astype(F32)).astype(BF)
@@ -512,12 +535,13 @@
         scratch_shapes=[
             pltpu.VMEM((FRAME, 4, 8, SLICE), BF),
             pltpu.VMEM((SUP, FRAME, SLICE), BF),
+            pltpu.VMEM((FRAME // 8, 8, FRAME), BF),
             pltpu.VMEM((32, 2, 8, SLICE), BF),
             pltpu.VMEM((32, 2, 8, SLICE), BF),
             pltpu.VMEM((32, 1, 8, SLICE), BF),
             pltpu.VMEM((32, 1, 8, SLICE), BF),
             pltpu.VMEM((FRAME, FRAME), F32),
-            pltpu.VMEM((12, FUN, FRAME), F32),
+            pltpu.VMEM((12, FUN // 8, 8, FRAME), BF),
             pltpu.VMEM((3, FUN, FRAME), F32),
             pltpu.VMEM((3, FUN, FRAME), BF),
             pltpu.VMEM((12, FUN, FRAME), BF),
@@ -533,7 +557,7 @@
             pltpu.VMEM((FUN, 4, 8, 1024), BF),
             pltpu.VMEM((384, 1024), BF),
             pltpu.VMEM((FUN, 4, 8, 1024), BF),
-            dma((3, 4)), dma((4, 4)), dma((4,)), dma((4,)), dma((7,)), dma((7,)),
+            dma((3, 4)), dma((4, 4)), dma((10,)), dma((10,)), dma((7,)), dma((7,)),
             dma((9,)), dma((12,)), dma((11,)), dma((12,)), dma((4,)), dma((4,)),
             dma((3, 3, 3)), dma((4, 3, 3)), dma, dma((3, 3)),
         ],

time: 79.1 us -> 72 us (0.910)
  Pallas kernels: 74.9 us -> 67.8 us
    pallas_call x1, Pallas kernels: 74.9 us -> 67.8 us  [on_device(): pl.pallas_call(exchange_kernel, out_shape=(jax.ShapeDtypeStruct((FUN, 4,...]
where the time goes in v2:
time: 72 us; the launch traced here: 71.8 us
  Pallas kernels  67.8 us (94%)
  local copies, waits for them, and re-layouts  3.36 us (5%)
    pallas_call x1, Pallas kernels, on_device(): pl.pallas_call(exchange_kernel, out_shape=(jax.ShapeDtypeStruct((FUN, 4,...  67.8 us
    unnamed x4, local copies, waits for them, and re-layouts  3.36 us

profile of v2, /device:TPU:0, one launch (start us, length us, event | category | flops | bytes accessed | tf_op | source)
XLA Modules:
  0.0 71.8 jit_solution(4857097737106791289)
XLA Ops:
  0.6 67.8 %exchange.1 = (bf16[24,4,8,1024]{3,2,1,0:T(8,128)(2,1)}, f32[24,256]{1,0:T(8,128)}) custom-call(bf16[24,4,8,1024]{3,2,1,0:T(8,128)(2,1)} %bitcast.3, bf16[1024,1024]{1,0:T(8,128)(2,1)} %kinetic.1, f32[12,1024]{1,0:T(8,128)} %pot.1, s32[24,128]{1,0:T(8,128)} %bitcast.5), custom_call_target="tpu_custom_call" | custom-call | tf_op jit(solution)/shard_map/exchange/pallas_call | solution.py:527
  68.4 0.0 copy-start
  68.4 2.7 %copy.8 = bf16[24,32,1024]{2,1,0:T(8,128)(2,1)} copy(bf16[24,32,1024]{2,1,0:T(8,128)(2,1)} %bitcast.4) | data formatting | bytes 3145728
  71.2 0.0 copy-done
  71.2 0.6 copy.9
Async XLA Ops:
  68.4 2.8 %copy-start = (f32[24,256]{1,0:T(8,128)S(1)}, f32[24,256]{1,0:T(8,128)}, u32[]{:S(2)}) copy-start(f32[24,256]{1,0:T(8,128)} %get-tuple-element.9) | copy-start | bytes 73732

commit v3 on v2

--- a/solution.py
+++ b/solution.py
@@ -44,9 +44,9 @@
 
 
 def exchange_kernel(
-    coeffs, kinetic, pot, lanes_in, out, gram_out,
+    coeffs, kinetic, pot_hbm, lanes_hbm, out, gram_hbm,
     frame, slots, gram_out_rows, back_a, back_b, back_c, back_d, gram, terms, sums, rows_out, rows_in, mixing, potb, boxes,
-    meta, starts, kin, v_win, pot_rows, pot_own, y_in, x_in, y_res,
+    pot, lanes_in, gram_out, meta, starts, kin, v_win, pot_rows, pot_own, y_in, x_in, y_res,
     y_send, y_recv, x_send, x_recv, v_send, v_recv, s_send, s_recv, c_send, c_recv, bx_send, bx_recv,
     by_send, by_recv, kin_sem, out_sem,
 ):
@@ -63,17 +63,13 @@
     for partner in partners:
         pl.semaphore_signal(barrier, inc=1, device_id=dev(partner), device_id_type=MESH)
 
-    kin_copy = pltpu.make_async_copy(kinetic, kin, kin_sem)
-    kin_copy.start()
-
-    frame[16:48, 0:3] = jnp.zeros((32, 3, 8, SLICE), BF)
-    frame[48:80, 0:2] = jnp.zeros((32, 2, 8, SLICE), BF)
-    frame[176:208, 2:4] = jnp.zeros((32, 2, 8, SLICE), BF)
-    frame[208:240, 1:4] = jnp.zeros((32, 3, 8, SLICE), BF)
-    slots[:, 0:16, :] = jnp.zeros((SUP, 16, SLICE), BF)
-    slots[:, 240:256, :] = jnp.zeros((SUP, 16, SLICE), BF)
-    potb[0:BOX, :] = pot[...].astype(BF)
-    potb[BOX:16, :] = jnp.zeros((16 - BOX, 1024), BF)
+    loads = [
+        pltpu.make_async_copy(src, dst, kin_sem.at[n])
+        for n, (src, dst) in enumerate(((lanes_hbm, lanes_in), (pot_hbm, pot), (kinetic, kin)))
+    ]
+    for copy in loads:
+        copy.start()
+
     pl.semaphore_wait(barrier, len(partners))
 
     started = []
@@ -103,6 +99,14 @@
             y_recv.at[y, q],
         ).start()
 
+    frame[16:48, 0:3] = jnp.zeros((32, 3, 8, SLICE), BF)
+    frame[48:80, 0:2] = jnp.zeros((32, 2, 8, SLICE), BF)
+    frame[176:208, 2:4] = jnp.zeros((32, 2, 8, SLICE), BF)
+    frame[208:240, 1:4] = jnp.zeros((32, 3, 8, SLICE), BF)
+    slots[:, 0:16, :] = jnp.zeros((SUP, 16, SLICE), BF)
+    slots[:, 240:256, :] = jnp.zeros((SUP, 16, SLICE), BF)
+
+    loads[0].wait()
     ring = lax.div(me, RING)
     flat = ring * OWN - LEFT + FUN_ALL
     top_line = lax.div(flat, 128)
@@ -205,6 +209,9 @@
         for q in range(4):
             wait_piece(ys, q)
 
+    loads[1].wait()
+    potb[0:BOX, :] = pot[...].astype(BF)
+    potb[BOX:16, :] = jnp.zeros((16 - BOX, 1024), BF)
     v_copies = []
     for o in range(-2, 5):
         if o == 0:
@@ -249,7 +256,11 @@
     lax.fori_loop(0, SUP // 4, gram_step, 0)
     scaled = gram[...] * VOLUME
     gram[...] = scaled
-    gram_out_rows[...] = scaled.reshape(FRAME // 8, 8, FRAME).astype(BF)
+    high_part = scaled.astype(BF)
+    rest = scaled - high_part.astype(F32)
+    rest = jnp.sum(jnp.where(row_id == col_id, rest, 0.0), axis=1, keepdims=True)
+    travels = jnp.where(col_id == FRAME - 1, rest, scaled)
+    gram_out_rows[...] = travels.reshape(FRAME // 8, 8, FRAME).astype(BF)
 
     s_copies = []
 
@@ -315,6 +326,14 @@
             wait_terms(8 + ys)
         sums[2] = arrived_terms(8) + arrived_terms(9) + arrived_terms(10) + arrived_terms(11)
 
+    short_lane = lax.broadcasted_iota(jnp.int32, (FUN, FRAME), 1)
+    short_sub = lax.broadcasted_iota(jnp.int32, (FUN, FRAME), 0)
+    for n, at in enumerate((176, LEFT, -16)):
+        held = sums[n]
+        low_part = held[:, FRAME - 1 : FRAME]
+        held = held + jnp.where(short_lane == short_sub + (FUN * y + at), low_part, 0.0)
+        sums[n] = jnp.where(short_lane == FRAME - 1, 0.0, held)
+
     pad = jnp.zeros((FUN, FRAME), F32)
     wide = jnp.concatenate([sums[0], pad], axis=1)
     wide += pltpu.roll(jnp.concatenate([sums[1], pad], axis=1), 96, 1)
@@ -359,6 +378,8 @@
         moved = pltpu.roll(band, 512 - (1 << bit), 1)
         band = jnp.where(jnp.bitwise_and(sub, 1 << bit) != 0, moved, band)
     gram_out[...] = jnp.where(lane[:, 0:256] == 255, 0.0, band[:, 0:256])
+    gram_copy = pltpu.make_async_copy(gram_out, gram_hbm, kin_sem.at[3])
+    gram_copy.start()
 
     def wait_rows(slot):
         pltpu.make_async_copy(rows_in.at[slot], rows_in.at[slot], c_recv.at[slot]).wait()
@@ -402,11 +423,10 @@
             frame[pl.ds(pl.multiple_of(8 * octet, 8), 8)] = out.reshape(8, 4, 8, SLICE).astype(BF)
         return carry
 
-    pairs(out_of_slots, 1, 4, W_HALO)
-    pairs(out_of_slots, 11, 4, W_HALO)
     backs = (back_a, back_b, back_c, back_d)
     x_backs = []
     for n, (src, q, nq, dst, to) in enumerate(HALO):
+        pairs(out_of_slots, dst // 16, 2, 2)
         copy = pltpu.make_async_remote_copy(
             src_ref=frame.at[pl.ds(dst, 32), pl.ds(q, nq)],
             dst_ref=backs[n],
@@ -457,7 +477,7 @@
         frame[src : src + 32, q : q + nq] = (mine + backs[n][...].astype(F32)).astype(BF)
     send_home(1)
 
-    kin_copy.wait()
+    loads[2].wait()
     out_copies = []
     for which in range(2):
         for j in range(3):
@@ -518,11 +538,11 @@
         copy.wait_send()
     for copy in out_copies:
         copy.wait()
+    gram_copy.wait()
 
 
 def on_device(coeffs, centers, kinetic, potential):
     hbm = pl.BlockSpec(memory_space=pl.ANY)
-    vmem = pl.BlockSpec(memory_space=pltpu.VMEM)
     dma = pltpu.SemaphoreType.DMA
     filtered, gram_band = pl.pallas_call(
         exchange_kernel,
@@ -530,8 +550,8 @@
             jax.ShapeDtypeStruct((FUN, 4, 8, 1024), BF),
             jax.ShapeDtypeStruct((FUN, FRAME), F32),
         ),
-        in_specs=[hbm, hbm, vmem, vmem],
-        out_specs=(hbm, vmem),
+        in_specs=[hbm, hbm, hbm, hbm],
+        out_specs=(hbm, hbm),
         scratch_shapes=[
             pltpu.VMEM((FRAME, 4, 8, SLICE), BF),
             pltpu.VMEM((SUP, FRAME, SLICE), BF),
@@ -548,6 +568,9 @@
             pltpu.VMEM((FRAME, FRAME), F32),
             pltpu.VMEM((16, 1024), BF),
             pltpu.VMEM((FRAME, 128), jnp.int32),
+            pltpu.VMEM((BOX, 1024), F32),
+            pltpu.VMEM((FUN, 128), jnp.int32),
+            pltpu.VMEM((FUN, FRAME), F32),
             pltpu.VMEM((64, FRAME), jnp.int32),
             pltpu.VMEM((32, FRAME), jnp.int32),
             pltpu.VMEM((1024, 1024), BF),
@@ -559,7 +582,7 @@
             pltpu.VMEM((FUN, 4, 8, 1024), BF),
             dma((3, 4)), dma((4, 4)), dma((10,)), dma((10,)), dma((7,)), dma((7,)),
             dma((9,)), dma((12,)), dma((11,)), dma((12,)), dma((4,)), dma((4,)),
-            dma((3, 3, 3)), dma((4, 3, 3)), dma, dma((3, 3)),
+            dma((3, 3, 3)), dma((4, 3, 3)), dma((4,)), dma((3, 3)),
         ],
         compiler_params=pltpu.CompilerParams(collective_id=0, has_side_effects=True),
         name="exchange",

time: 72 us -> 70.4 us (0.978)
  Pallas kernels: 67.8 us -> 66.3 us
    pallas_call x1, Pallas kernels: 67.8 us -> 66.3 us  [on_device(): pl.pallas_call(exchange_kernel, out_shape=(jax.ShapeDtypeStruct((FUN, 4,...]
where the time goes in v3:
time: 70.4 us; the launch traced here: 70.3 us
  Pallas kernels  66.3 us (94%)
  local copies, waits for them, and re-layouts  3.36 us (5%)
    pallas_call x1, Pallas kernels, on_device(): pl.pallas_call(exchange_kernel, out_shape=(jax.ShapeDtypeStruct((FUN, 4,...  66.3 us
    unnamed x4, local copies, waits for them, and re-layouts  3.36 us

profile of v3, /device:TPU:0, one launch (start us, length us, event | category | flops | bytes accessed | tf_op | source)
XLA Modules:
  0.0 70.3 jit_solution(15114195359569657620)
XLA Ops:
  0.6 66.3 %exchange.1 = (bf16[24,4,8,1024]{3,2,1,0:T(8,128)(2,1)}, f32[24,256]{1,0:T(8,128)}) custom-call(bf16[24,4,8,1024]{3,2,1,0:T(8,128)(2,1)} %bitcast.3, bf16[1024,1024]{1,0:T(8,128)(2,1)} %kinetic.1, f32[12,1024]{1,0:T(8,128)} %pot_hbm.1, s32[24,128]{1,0:T(8,128)} %bitcast.5), custom_call_target="tpu_custom_call" | custom-call | tf_op jit(solution)/shard_map/exchange/pallas_call | solution.py:547
  66.9 0.0 copy-start
  66.9 2.7 %copy.8 = bf16[24,32,1024]{2,1,0:T(8,128)(2,1)} copy(bf16[24,32,1024]{2,1,0:T(8,128)(2,1)} %bitcast.4) | data formatting | bytes 3145728
  69.7 0.0 copy-done
  69.7 0.6 copy.9
Async XLA Ops:
  66.9 2.8 %copy-start = (f32[24,256]{1,0:T(8,128)S(1)}, f32[24,256]{1,0:T(8,128)}, u32[]{:S(2)}) copy-start(f32[24,256]{1,0:T(8,128)} %get-tuple-element.9) | copy-start | bytes 73732

commit v4 on v3

--- a/solution.py
+++ b/solution.py
@@ -44,11 +44,11 @@
 
 
 def exchange_kernel(
-    coeffs, kinetic, pot_hbm, lanes_hbm, out, gram_hbm,
+    coeffs, kinetic, pot_hbm, lanes_hbm, y_res, gram_out,
     frame, slots, gram_out_rows, back_a, back_b, back_c, back_d, gram, terms, sums, rows_out, rows_in, mixing, potb, boxes,
-    pot, lanes_in, gram_out, meta, starts, kin, v_win, pot_rows, pot_own, y_in, x_in, y_res,
+    pot, lanes_in, meta, starts, kin, v_win, pot_rows, pot_own, y_in, x_in,
     y_send, y_recv, x_send, x_recv, v_send, v_recv, s_send, s_recv, c_send, c_recv, bx_send, bx_recv,
-    by_send, by_recv, kin_sem, out_sem,
+    by_send, by_recv, kin_sem,
 ):
     me = lax.axis_index("func") * 16 + lax.axis_index("box")
     y = lax.rem(me, RING)
@@ -359,10 +359,6 @@
         copy.start()
         return copy
 
-    own_rows = [
-        send_rows(k - 1, 1, 4 + y, base + lax.rem(y + k, RING)) for k in range(1, 4)
-    ]
-
     @pl.when(y <= 2)
     def _():
         for yp in range(RING):
@@ -372,14 +368,16 @@
     def _():
         for yp in range(RING):
             send_rows(7 + yp, 2, y, base + RING + yp)
+
+    own_rows = [
+        send_rows(k - 1, 1, 4 + y, base + lax.rem(y + k, RING)) for k in range(1, 4)
+    ]
 
     band = pltpu.roll(wide, 512 - 49 - FUN * y, 1)
     for bit in range(5):
         moved = pltpu.roll(band, 512 - (1 << bit), 1)
         band = jnp.where(jnp.bitwise_and(sub, 1 << bit) != 0, moved, band)
     gram_out[...] = jnp.where(lane[:, 0:256] == 255, 0.0, band[:, 0:256])
-    gram_copy = pltpu.make_async_copy(gram_out, gram_hbm, kin_sem.at[3])
-    gram_copy.start()
 
     def wait_rows(slot):
         pltpu.make_async_copy(rows_in.at[slot], rows_in.at[slot], c_recv.at[slot]).wait()
@@ -425,7 +423,10 @@
 
     backs = (back_a, back_b, back_c, back_d)
     x_backs = []
-    for n, (src, q, nq, dst, to) in enumerate(HALO):
+    lanes = pl.ds(pl.multiple_of(y * SLICE, SLICE), SLICE)
+
+    def halo_back(n):
+        src, q, nq, dst, to = HALO[n]
         pairs(out_of_slots, dst // 16, 2, 2)
         copy = pltpu.make_async_remote_copy(
             src_ref=frame.at[pl.ds(dst, 32), pl.ds(q, nq)],
@@ -437,80 +438,91 @@
         )
         copy.start()
         x_backs.append(copy)
-    pairs(out_of_slots, 5, 6, W_OWN)
-
-    lanes = pl.ds(pl.multiple_of(y * SLICE, SLICE), SLICE)
-    y_backs = []
-
-    def quarters(octet):
-        unit = lax.div(octet, 4)
-        clean = 2 - unit
-        first = 2 * lax.div(unit, 2)
-        second = 3 - 2 * lax.div(3 - unit, 3)
-        return ((clean, 2),), ((first, 1), (second, 1))
-
-    def send_home(which):
-        for k in (1, 3, 2, 0):
-            yp = lax.rem(y + k, RING)
-            for j in range(3):
-                for n, (q, nq) in enumerate(quarters(3 * yp + j)[which]):
-                    src = frame.at[pl.ds(pl.multiple_of(LEFT + FUN * yp + 8 * j, 8), 8), pl.ds(q, nq)]
-                    dst = y_in.at[pl.ds(8 * j, 8), pl.ds(q, nq), :, lanes]
-                    if k == 0:
-                        pltpu.make_async_copy(src, dst, by_recv.at[y, j, which + n]).start()
-                        continue
-                    copy = pltpu.make_async_remote_copy(
-                        src_ref=src,
-                        dst_ref=dst,
-                        send_sem=by_send.at[k - 1, j, which + n],
-                        recv_sem=by_recv.at[y, j, which + n],
-                        device_id=dev(base + yp),
-                        device_id_type=MESH,
-                    )
-                    copy.start()
-                    y_backs.append(copy)
-
-    send_home(0)
-    for n, (src, q, nq, dst, to) in enumerate(HALO):
+
+    def merge(n):
+        src, q, nq, dst, to = HALO[n]
         x_backs[n].wait_recv()
         mine = frame[src : src + 32, q : q + nq].astype(F32)
         frame[src : src + 32, q : q + nq] = (mine + backs[n][...].astype(F32)).astype(BF)
-    send_home(1)
+
+    def quarters(octet):
+        unit = octet // 4 if isinstance(octet, int) else lax.div(octet, 4)
+        half = (unit + 1) // 3 if isinstance(octet, int) else lax.div(unit + 1, 3)
+        late = (unit + 2) // 3 if isinstance(octet, int) else lax.div(unit + 2, 3)
+        return ((2 - unit, 2),), ((2 * half, 1), (1 + 2 * late, 1))
+
+    def home_part(octet, n, which):
+        q, nq = quarters(octet)[which][n]
+        return frame.at[pl.ds(LEFT + 8 * octet, 8), pl.ds(q, nq)]
+
+    def send_home(octets, which):
+        for octet in octets:
+            yp, j = octet // 3, octet % 3
+            for n, (q, nq) in enumerate(quarters(octet)[which]):
+                src = home_part(octet, n, which)
+                dst = y_in.at[pl.ds(8 * j, 8), pl.ds(q, nq), :, lanes]
+                kind = which + n
+
+                @pl.when(y != yp)
+                def _():
+                    pltpu.make_async_remote_copy(
+                        src_ref=src,
+                        dst_ref=dst,
+                        send_sem=by_send.at[octet, kind],
+                        recv_sem=by_recv.at[y, j, kind],
+                        device_id=dev(base + yp),
+                        device_id_type=MESH,
+                    ).start()
+
+                @pl.when(y == yp)
+                def _():
+                    pltpu.make_async_copy(src, dst, by_recv.at[y, j, kind]).start()
+
+    pairs(out_of_slots, 5, 3, 3)
+    send_home(range(0, 6), 0)
+    halo_back(0)
+    halo_back(1)
+    pairs(out_of_slots, 8, 3, 3)
+    send_home(range(6, 12), 0)
+    halo_back(2)
+    halo_back(3)
+    merge(0)
+    send_home(range(0, 4), 1)
+    merge(1)
+    send_home(range(8, 12), 1)
+    merge(2)
+    merge(3)
+    send_home(range(4, 8), 1)
 
     loads[2].wait()
-    out_copies = []
     for which in range(2):
+        for k in (0, 1, 3, 2):
+            ys = lax.rem(y + k, RING)
+            cols = pl.ds(pl.multiple_of(ys * SLICE, SLICE), SLICE)
+            for j in range(3):
+                for n, (q, nq) in enumerate(quarters(3 * y + j)[which]):
+                    part = y_in.at[pl.ds(8 * j, 8), pl.ds(q, nq), :, cols]
+                    pltpu.make_async_copy(part, part, by_recv.at[ys, j, which + n]).wait()
+            held, local = [], []
+            for j in range(3):
+                for n, (q, nq) in enumerate(quarters(3 * y + j)[which]):
+                    part = (slice(8 * j, 8 * j + 8), pl.ds(q, nq), slice(None), cols)
+                    held.append(y_in[part].astype(F32).reshape(64 * nq, SLICE))
+                    local.append(pot_own[part].reshape(64 * nq, SLICE))
+            held = jnp.concatenate(held, axis=0)
+            local = jnp.concatenate(local, axis=0)
+            applied = jnp.dot(held.astype(BF), kin[cols, :], preferred_element_type=F32)
+            if k == 0:
+                x_in[...] = applied
+            else:
+                x_in[...] += applied
+            x_in[:, cols] += local * held
+        at = 0
         for j in range(3):
-            octs = quarters(3 * y + j)[which]
-            for n, (q, nq) in enumerate(octs):
-                for ys in range(RING):
-                    part = y_in.at[pl.ds(8 * j, 8), pl.ds(q, nq), :, pl.ds(ys * SLICE, SLICE)]
-                    pltpu.make_async_copy(part, part, by_recv.at[ys, j, which + n]).wait()
-                rows = 8 * 8 * nq
-                at = 128 * j + rows * n
-                piece = y_in[8 * j : 8 * j + 8, pl.ds(q, nq)].astype(F32).reshape(rows, 1024)
-                x_in[at : at + rows, :] = piece.astype(BF)
-        for t in range(4):
-            cols = slice(256 * t, 256 * t + 256)
-            applied = jnp.dot(x_in[...], kin[:, cols], preferred_element_type=F32)
-            for j in range(3):
-                octs = quarters(3 * y + j)[which]
-                for n, (q, nq) in enumerate(octs):
-                    rows = 8 * 8 * nq
-                    at = 128 * j + rows * n
-                    local = pot_own[8 * j : 8 * j + 8, pl.ds(q, nq), :, cols].reshape(rows, 256)
-                    res = applied[at : at + rows] + local * x_in[at : at + rows, cols].astype(F32)
-                    y_res[8 * j : 8 * j + 8, pl.ds(q, nq), :, cols] = res.reshape(8, nq, 8, 256).astype(BF)
-        for j in range(3):
-            octs = quarters(3 * y + j)[which]
-            for n, (q, nq) in enumerate(octs):
-                copy = pltpu.make_async_copy(
-                    y_res.at[pl.ds(8 * j, 8), pl.ds(q, nq)],
-                    out.at[pl.ds(8 * j, 8), pl.ds(q, nq)],
-                    out_sem.at[j, which + n],
-                )
-                copy.start()
-                out_copies.append(copy)
+            for n, (q, nq) in enumerate(quarters(3 * y + j)[which]):
+                piece = x_in[at : at + 64 * nq, :].astype(BF).astype(F32)
+                y_res[8 * j : 8 * j + 8, pl.ds(q, nq)] = piece.reshape(8, nq, 8, 1024).astype(BF)
+                at += 64 * nq
 
     for copy in started:
         copy.wait_send()
@@ -534,24 +546,39 @@
 
     for copy in x_backs:
         copy.wait_send()
-    for copy in y_backs:
-        copy.wait_send()
-    for copy in out_copies:
+    for octet in range(12):
+        for which in range(2):
+            for n in range(which + 1):
+                part = home_part(octet, n, which)
+
+                @pl.when(y != octet // 3)
+                def _():
+                    pltpu.make_async_copy(part, part, by_send.at[octet, which + n]).wait()
+
+
+def write_kernel(pieces, rows, pieces_out, rows_out, sem):
+    copies = [
+        pltpu.make_async_copy(pieces, pieces_out, sem.at[0]),
+        pltpu.make_async_copy(rows, rows_out, sem.at[1]),
+    ]
+    for copy in copies:
+        copy.start()
+    for copy in copies:
         copy.wait()
-    gram_copy.wait()
 
 
 def on_device(coeffs, centers, kinetic, potential):
     hbm = pl.BlockSpec(memory_space=pl.ANY)
+    vmem = pl.BlockSpec(memory_space=pltpu.VMEM)
     dma = pltpu.SemaphoreType.DMA
-    filtered, gram_band = pl.pallas_call(
+    results = pl.pallas_call(
         exchange_kernel,
         out_shape=(
-            jax.ShapeDtypeStruct((FUN, 4, 8, 1024), BF),
-            jax.ShapeDtypeStruct((FUN, FRAME), F32),
+            pltpu.VMEM((FUN, 4, 8, 1024), BF),
+            pltpu.VMEM((FUN, FRAME), F32),
         ),
         in_specs=[hbm, hbm, hbm, hbm],
-        out_specs=(hbm, hbm),
+        out_specs=(vmem, vmem),
         scratch_shapes=[
             pltpu.VMEM((FRAME, 4, 8, SLICE), BF),
             pltpu.VMEM((SUP, FRAME, SLICE), BF),
@@ -570,7 +597,6 @@
             pltpu.VMEM((FRAME, 128), jnp.int32),
             pltpu.VMEM((BOX, 1024), F32),
             pltpu.VMEM((FUN, 128), jnp.int32),
-            pltpu.VMEM((FUN, FRAME), F32),
             pltpu.VMEM((64, FRAME), jnp.int32),
             pltpu.VMEM((32, FRAME), jnp.int32),
             pltpu.VMEM((1024, 1024), BF),
@@ -578,15 +604,25 @@
             pltpu.VMEM((128, 1024), F32),
             pltpu.VMEM((FUN, 4, 8, 1024), F32),
             pltpu.VMEM((FUN, 4, 8, 1024), BF),
-            pltpu.VMEM((384, 1024), BF),
-            pltpu.VMEM((FUN, 4, 8, 1024), BF),
+            pltpu.VMEM((384, 1024), F32),
             dma((3, 4)), dma((4, 4)), dma((10,)), dma((10,)), dma((7,)), dma((7,)),
             dma((9,)), dma((12,)), dma((11,)), dma((12,)), dma((4,)), dma((4,)),
-            dma((3, 3, 3)), dma((4, 3, 3)), dma((4,)), dma((3, 3)),
+            dma((12, 3)), dma((4, 3, 3)), dma((3,)),
         ],
         compiler_params=pltpu.CompilerParams(collective_id=0, has_side_effects=True),
         name="exchange",
     )(coeffs.reshape(FUN, 4, 8, 1024), kinetic, potential, centers.reshape(FUN, 128))
+    filtered, gram_band = pl.pallas_call(
+        write_kernel,
+        out_shape=(
+            jax.ShapeDtypeStruct((FUN, 4, 8, 1024), BF),
+            jax.ShapeDtypeStruct((FUN, FRAME), F32),
+        ),
+        in_specs=[vmem, vmem],
+        out_specs=(hbm, hbm),
+        scratch_shapes=[dma((2,))],
+        name="write",
+    )(*[pltpu.with_memory_space_constraint(r, pltpu.VMEM) for r in results])
     return filtered.reshape(FUN, SUP, 1024), gram_band
 
 

time: 70.4 us -> 65.9 us (0.936)
  local copies, waits for them, and re-layouts: 3.36 us -> 0 us
  Pallas kernels: 66.3 us -> 65.1 us
    unnamed x4 -> x0, local copies, waits for them, and re-layouts: 3.36 us -> none
    pallas_call x1 -> x2, Pallas kernels: 66.3 us -> 65.1 us  [the longest x1 63.9 us: on_device(): pl.pallas_call(exchange_kernel, out_shape=(pltpu.VMEM((FUN, 4, 8, 1024),...]
where the time goes in v4:
time: 65.9 us; the launch traced here: 65.7 us
  Pallas kernels  65.1 us (99%)
    pallas_call x1, Pallas kernels, on_device(): pl.pallas_call(exchange_kernel, out_shape=(pltpu.VMEM((FUN, 4, 8, 1024),...  63.9 us

profile of v4, /device:TPU:0, one launch (start us, length us, event | category | flops | bytes accessed | tf_op | source)
XLA Modules:
  0.0 65.7 jit_solution(11930965351090656951)
XLA Ops:
  0.6 63.9 %exchange.1 = (bf16[24,4,8,1024]{3,2,1,0:T(8,128)(2,1)S(1)}, f32[24,256]{1,0:T(8,128)S(1)}) custom-call(bf16[24,4,8,1024]{3,2,1,0:T(8,128)(2,1)} %bitcast.3, bf16[1024,1024]{1,0:T(8,128)(2,1)} %kinetic.1, f32[12,1024]{1,0:T(8,128)} %pot_hbm.1, s32[24,128]{1,0:T(8,128)} %bitcast.4), custom_call_target="tpu_custom_call" | custom-call | tf_op jit(solution)/shard_map/exchange/pallas_call | solution.py:574
  64.6 1.2 %write.1 = (bf16[24,4,8,1024]{3,2,1,0:T(8,128)(2,1)}, f32[24,256]{1,0:T(8,128)}) custom-call(bf16[24,4,8,1024]{3,2,1,0:T(8,128)(2,1)S(1)} %get-tuple-element.6.pieces, f32[24,256]{1,0:T(8,128)S(1)} %get-tuple-element.7.rows), custom_call_target="tpu_custom_call" | custom-call | tf_op jit(solution)/shard_map/write/pallas_call | solution.py:615

commit v5 on v4

--- a/solution.py
+++ b/solution.py
@@ -21,6 +21,7 @@
 FUN_ALL = 3072
 W_HALO = 4
 W_OWN = 6
+LIVE = slice(16, 240)
 VOLUME = 1.0 / (32 * 1024)
 
 HALO = (
@@ -81,7 +82,7 @@
     for p in range(4):
         q0 = p + inner * ((0, 3, 1, 2)[p] - p)
         q = q0 + high * (3 - 2 * q0)
-        for k in (1, 3, 2):
+        for k in (2, 1, 3):
             yp = lax.rem(y + k, RING)
             copy = pltpu.make_async_remote_copy(
                 src_ref=coeffs.at[:, q, :, pl.ds(pl.multiple_of(yp * SLICE, SLICE), SLICE)],
@@ -209,6 +210,158 @@
         for q in range(4):
             wait_piece(ys, q)
 
+    pairs(into_slots, 5, 6, W_OWN)
+
+    def same_box(slot):
+        box_row = rel_row + jnp.bitwise_and(slot - rel_row, SUP - 1)
+        owned = jnp.logical_and(box_row >= low_row, box_row <= top_row)
+        box_row = jnp.where(owned, box_row, -1)
+        col = boxes[LIVE, :]
+        box_col = col + jnp.bitwise_and(slot - col, SUP - 1)
+        return box_col == box_row[:, 0:128], box_col == box_row[:, 128:256]
+
+    gram[...] = jnp.zeros((FRAME, FRAME), F32)
+
+    def gram_step(step, carry):
+        lo, hi = gram[LIVE, 0:128], gram[LIVE, 128:256]
+        for part in range(4):
+            slot = 4 * step + part
+            held = slots[slot]
+            prod = lax.dot_general(held[LIVE], held, (((1,), (1,)), ((), ())), preferred_element_type=F32)
+            same_lo, same_hi = same_box(slot)
+            lo = lo + jnp.where(same_lo, prod[:, 0:128], 0.0)
+            hi = hi + jnp.where(same_hi, prod[:, 128:256], 0.0)
+        gram[LIVE, 0:128] = lo
+        gram[LIVE, 128:256] = hi
+        return carry
+
+    lax.fori_loop(0, SUP // 4, gram_step, 0)
+    scaled = gram[...] * VOLUME
+    gram[...] = scaled
+    high_part = scaled.astype(BF)
+    rest = scaled - high_part.astype(F32)
+    rest = jnp.sum(jnp.where(row_id == col_id, rest, 0.0), axis=1, keepdims=True)
+    travels = jnp.where(col_id == FRAME - 1, rest, scaled)
+    gram_out_rows[...] = travels.reshape(FRAME // 8, 8, FRAME).astype(BF)
+
+    s_copies = []
+
+    def send_terms(n, start, slot, target):
+        copy = pltpu.make_async_remote_copy(
+            src_ref=gram_out_rows.at[pl.ds(start, FUN // 8)],
+            dst_ref=terms.at[slot],
+            send_sem=s_send.at[n],
+            recv_sem=s_recv.at[slot],
+            device_id=dev(target),
+            device_id_type=MESH,
+        )
+        copy.start()
+        s_copies.append(copy)
+
+    for yp in range(1, 4):
+        send_terms(2 + yp, 3 * yp - 2, 8 + y, base - RING + yp)
+    for yp in range(0, 3):
+        send_terms(6 + yp, 22 + 3 * yp, y, base + RING + yp)
+    for k in range(1, 4):
+        yp = lax.rem(y + k, RING)
+        send_terms(k - 1, LEFT // 8 + 3 * yp, 4 + y, base + yp)
+
+    def wait_terms(slot):
+        pltpu.make_async_copy(terms.at[slot], terms.at[slot], s_recv.at[slot]).wait()
+
+    def arrived_terms(slot):
+        return terms[slot].astype(F32).reshape(FUN, FRAME)
+
+    sums[0] = jnp.zeros((FUN, FRAME), F32)
+    sums[2] = jnp.zeros((FUN, FRAME), F32)
+    sums[1] = gram[my_rows, :]
+    for k in range(1, 4):
+        slot = 4 + lax.rem(y + k, RING)
+        wait_terms(slot)
+        sums[1] += arrived_terms(slot)
+
+    @pl.when(y <= 2)
+    def _():
+        for ys in range(RING):
+            wait_terms(ys)
+        sums[0] = arrived_terms(0) + arrived_terms(1) + arrived_terms(2) + arrived_terms(3)
+
+    @pl.when(y >= 1)
+    def _():
+        for ys in range(RING):
+            wait_terms(8 + ys)
+        sums[2] = arrived_terms(8) + arrived_terms(9) + arrived_terms(10) + arrived_terms(11)
+
+    short_lane = lax.broadcasted_iota(jnp.int32, (FUN, FRAME), 1)
+    short_sub = lax.broadcasted_iota(jnp.int32, (FUN, FRAME), 0)
+    for n, at in enumerate((176, LEFT, -16)):
+        held = sums[n]
+        low_part = held[:, FRAME - 1 : FRAME]
+        held = held + jnp.where(short_lane == short_sub + (FUN * y + at), low_part, 0.0)
+        sums[n] = jnp.where(short_lane == FRAME - 1, 0.0, held)
+
+    pad = jnp.zeros((FUN, FRAME), F32)
+    wide = jnp.concatenate([sums[0], pad], axis=1)
+    wide += pltpu.roll(jnp.concatenate([sums[1], pad], axis=1), 96, 1)
+    wide += pltpu.roll(jnp.concatenate([sums[2], pad], axis=1), 192, 1)
+    lane = lax.broadcasted_iota(jnp.int32, (FUN, 512), 1)
+    sub = lax.broadcasted_iota(jnp.int32, (FUN, 512), 0)
+    fixed = (1.5 * (lane == sub + (FUN * y + 176)).astype(F32) - 0.5 * wide)
+    rows_out[0] = fixed[:, 0:256].astype(BF)
+    rows_out[1] = pltpu.roll(fixed, 512 - 96, 1)[:, 0:256].astype(BF)
+    rows_out[2] = pltpu.roll(fixed, 512 - 192, 1)[:, 0:256].astype(BF)
+
+    c_copies = []
+
+    def send_rows(n, which, slot, target):
+        copy = pltpu.make_async_remote_copy(
+            src_ref=rows_out.at[which],
+            dst_ref=rows_in.at[slot],
+            send_sem=c_send.at[n],
+            recv_sem=c_recv.at[slot],
+            device_id=dev(target),
+            device_id_type=MESH,
+        )
+        copy.start()
+        return copy
+
+    @pl.when(y <= 2)
+    def _():
+        for yp in range(RING):
+            send_rows(3 + yp, 0, 8 + y, base - RING + yp)
+
+    @pl.when(y >= 1)
+    def _():
+        for yp in range(RING):
+            send_rows(7 + yp, 2, y, base + RING + yp)
+
+    own_rows = [
+        send_rows(k - 1, 1, 4 + y, base + lax.rem(y + k, RING)) for k in range(1, 4)
+    ]
+
+    band = pltpu.roll(wide, 512 - 49 - FUN * y, 1)
+    for bit in range(5):
+        moved = pltpu.roll(band, 512 - (1 << bit), 1)
+        band = jnp.where(jnp.bitwise_and(sub, 1 << bit) != 0, moved, band)
+    gram_out[...] = jnp.where(lane[:, 0:256] == 255, 0.0, band[:, 0:256])
+
+    def wait_rows(slot):
+        pltpu.make_async_copy(rows_in.at[slot], rows_in.at[slot], c_recv.at[slot]).wait()
+
+    mixing[0:16, :] = jnp.zeros((16, FRAME), F32)
+    mixing[240:256, :] = jnp.zeros((16, FRAME), F32)
+    mixing[my_rows, :] = rows_out[1].astype(F32)
+    for k in range(1, 4):
+        ys = lax.rem(y + k, RING)
+        wait_rows(4 + ys)
+        mixing[pl.ds(pl.multiple_of(LEFT + FUN * ys, 8), FUN), :] = rows_in[4 + ys].astype(F32)
+    for ys in range(0, 3):
+        wait_rows(8 + ys)
+        mixing[176 + FUN * ys : 200 + FUN * ys, :] = rows_in[8 + ys].astype(F32)
+    for ys in range(1, 4):
+        wait_rows(ys)
+        mixing[FUN * ys - 16 : FUN * ys + 8, :] = rows_in[ys].astype(F32)
+
     loads[1].wait()
     potb[0:BOX, :] = pot[...].astype(BF)
     potb[BOX:16, :] = jnp.zeros((16 - BOX, 1024), BF)
@@ -228,182 +381,14 @@
         copy.start()
         v_copies.append(copy)
 
-    pairs(into_slots, 5, 6, W_OWN)
-
-    def same_box(slot):
-        box_row = rel_row + jnp.bitwise_and(slot - rel_row, SUP - 1)
-        owned = jnp.logical_and(box_row >= low_row, box_row <= top_row)
-        box_row = jnp.where(owned, box_row, -1)
-        col = boxes[...]
-        box_col = col + jnp.bitwise_and(slot - col, SUP - 1)
-        return box_col == box_row[:, 0:128], box_col == box_row[:, 128:256]
-
-    gram[...] = jnp.zeros((FRAME, FRAME), F32)
-
-    def gram_step(step, carry):
-        lo, hi = gram[:, 0:128], gram[:, 128:256]
-        for part in range(4):
-            slot = 4 * step + part
-            held = slots[slot]
-            prod = lax.dot_general(held, held, (((1,), (1,)), ((), ())), preferred_element_type=F32)
-            same_lo, same_hi = same_box(slot)
-            lo = lo + jnp.where(same_lo, prod[:, 0:128], 0.0)
-            hi = hi + jnp.where(same_hi, prod[:, 128:256], 0.0)
-        gram[:, 0:128] = lo
-        gram[:, 128:256] = hi
-        return carry
-
-    lax.fori_loop(0, SUP // 4, gram_step, 0)
-    scaled = gram[...] * VOLUME
-    gram[...] = scaled
-    high_part = scaled.astype(BF)
-    rest = scaled - high_part.astype(F32)
-    rest = jnp.sum(jnp.where(row_id == col_id, rest, 0.0), axis=1, keepdims=True)
-    travels = jnp.where(col_id == FRAME - 1, rest, scaled)
-    gram_out_rows[...] = travels.reshape(FRAME // 8, 8, FRAME).astype(BF)
-
-    s_copies = []
-
-    def send_terms(n, start, slot, target):
-        copy = pltpu.make_async_remote_copy(
-            src_ref=gram_out_rows.at[pl.ds(start, FUN // 8)],
-            dst_ref=terms.at[slot],
-            send_sem=s_send.at[n],
-            recv_sem=s_recv.at[slot],
-            device_id=dev(target),
-            device_id_type=MESH,
-        )
-        copy.start()
-        s_copies.append(copy)
-
-    for yp in range(1, 4):
-        send_terms(2 + yp, 3 * yp - 2, 8 + y, base - RING + yp)
-    for yp in range(0, 3):
-        send_terms(6 + yp, 22 + 3 * yp, y, base + RING + yp)
-    for k in range(1, 4):
-        yp = lax.rem(y + k, RING)
-        send_terms(k - 1, LEFT // 8 + 3 * yp, 4 + y, base + yp)
-
-    for copy in v_copies:
-        if copy is v_copies[2]:
-            copy.wait()
-        else:
-            copy.wait_recv()
-    for k in range(7):
-        pot_rows[BOX * k : BOX * k + BOX, :] = v_win[k].astype(F32)[0:BOX]
-    pot_rows[7 * BOX : 128, :] = jnp.zeros((128 - 7 * BOX, 1024), F32)
-
-    near_rows = pot_rows[...].astype(BF)
-    row_of = lax.broadcasted_iota(jnp.int32, (128, FRAME), 0)
-    for j in range(3):
-        select = (row_of == starts[pl.ds(LEFT // 8 + 3 * y + j, 1), :]).astype(F32).astype(BF)
-        local = lax.dot_general(select, near_rows, (((0,), (0,)), ((), ())), preferred_element_type=F32)
-        pot_own[8 * j : 8 * j + 8] = local.reshape(8, 4, 8, 1024)
-
-    def wait_terms(slot):
-        pltpu.make_async_copy(terms.at[slot], terms.at[slot], s_recv.at[slot]).wait()
-
-    def arrived_terms(slot):
-        return terms[slot].astype(F32).reshape(FUN, FRAME)
-
-    sums[0] = jnp.zeros((FUN, FRAME), F32)
-    sums[2] = jnp.zeros((FUN, FRAME), F32)
-    sums[1] = gram[my_rows, :]
-    for k in range(1, 4):
-        slot = 4 + lax.rem(y + k, RING)
-        wait_terms(slot)
-        sums[1] += arrived_terms(slot)
-
-    @pl.when(y <= 2)
-    def _():
-        for ys in range(RING):
-            wait_terms(ys)
-        sums[0] = arrived_terms(0) + arrived_terms(1) + arrived_terms(2) + arrived_terms(3)
-
-    @pl.when(y >= 1)
-    def _():
-        for ys in range(RING):
-            wait_terms(8 + ys)
-        sums[2] = arrived_terms(8) + arrived_terms(9) + arrived_terms(10) + arrived_terms(11)
-
-    short_lane = lax.broadcasted_iota(jnp.int32, (FUN, FRAME), 1)
-    short_sub = lax.broadcasted_iota(jnp.int32, (FUN, FRAME), 0)
-    for n, at in enumerate((176, LEFT, -16)):
-        held = sums[n]
-        low_part = held[:, FRAME - 1 : FRAME]
-        held = held + jnp.where(short_lane == short_sub + (FUN * y + at), low_part, 0.0)
-        sums[n] = jnp.where(short_lane == FRAME - 1, 0.0, held)
-
-    pad = jnp.zeros((FUN, FRAME), F32)
-    wide = jnp.concatenate([sums[0], pad], axis=1)
-    wide += pltpu.roll(jnp.concatenate([sums[1], pad], axis=1), 96, 1)
-    wide += pltpu.roll(jnp.concatenate([sums[2], pad], axis=1), 192, 1)
-    lane = lax.broadcasted_iota(jnp.int32, (FUN, 512), 1)
-    sub = lax.broadcasted_iota(jnp.int32, (FUN, 512), 0)
-    fixed = (1.5 * (lane == sub + (FUN * y + 176)).astype(F32) - 0.5 * wide)
-    rows_out[0] = fixed[:, 0:256].astype(BF)
-    rows_out[1] = pltpu.roll(fixed, 512 - 96, 1)[:, 0:256].astype(BF)
-    rows_out[2] = pltpu.roll(fixed, 512 - 192, 1)[:, 0:256].astype(BF)
-
-    c_copies = []
-
-    def send_rows(n, which, slot, target):
-        copy = pltpu.make_async_remote_copy(
-            src_ref=rows_out.at[which],
-            dst_ref=rows_in.at[slot],
-            send_sem=c_send.at[n],
-            recv_sem=c_recv.at[slot],
-            device_id=dev(target),
-            device_id_type=MESH,
-        )
-        copy.start()
-        return copy
-
-    @pl.when(y <= 2)
-    def _():
-        for yp in range(RING):
-            send_rows(3 + yp, 0, 8 + y, base - RING + yp)
-
-    @pl.when(y >= 1)
-    def _():
-        for yp in range(RING):
-            send_rows(7 + yp, 2, y, base + RING + yp)
-
-    own_rows = [
-        send_rows(k - 1, 1, 4 + y, base + lax.rem(y + k, RING)) for k in range(1, 4)
-    ]
-
-    band = pltpu.roll(wide, 512 - 49 - FUN * y, 1)
-    for bit in range(5):
-        moved = pltpu.roll(band, 512 - (1 << bit), 1)
-        band = jnp.where(jnp.bitwise_and(sub, 1 << bit) != 0, moved, band)
-    gram_out[...] = jnp.where(lane[:, 0:256] == 255, 0.0, band[:, 0:256])
-
-    def wait_rows(slot):
-        pltpu.make_async_copy(rows_in.at[slot], rows_in.at[slot], c_recv.at[slot]).wait()
-
-    mixing[0:16, :] = jnp.zeros((16, FRAME), F32)
-    mixing[240:256, :] = jnp.zeros((16, FRAME), F32)
-    mixing[my_rows, :] = rows_out[1].astype(F32)
-    for k in range(1, 4):
-        ys = lax.rem(y + k, RING)
-        wait_rows(4 + ys)
-        mixing[pl.ds(pl.multiple_of(LEFT + FUN * ys, 8), FUN), :] = rows_in[4 + ys].astype(F32)
-    for ys in range(0, 3):
-        wait_rows(8 + ys)
-        mixing[176 + FUN * ys : 200 + FUN * ys, :] = rows_in[8 + ys].astype(F32)
-    for ys in range(1, 4):
-        wait_rows(ys)
-        mixing[FUN * ys - 16 : FUN * ys + 8, :] = rows_in[ys].astype(F32)
-
     def mix_step(step, carry):
         for part in range(4):
             slot = 4 * step + part
             same_lo, same_hi = same_box(slot)
             mix = jnp.concatenate(
-                [jnp.where(same_lo, mixing[:, 0:128], 0.0), jnp.where(same_hi, mixing[:, 128:256], 0.0)], axis=1
+                [jnp.where(same_lo, mixing[LIVE, 0:128], 0.0), jnp.where(same_hi, mixing[LIVE, 128:256], 0.0)], axis=1
             ).astype(BF)
-            slots[slot] = jnp.dot(mix, slots[slot], preferred_element_type=F32).astype(BF)
+            slots[slot, LIVE, :] = jnp.dot(mix, slots[slot], preferred_element_type=F32).astype(BF)
         return carry
 
     lax.fori_loop(0, SUP // 4, mix_step, 0)
@@ -478,14 +463,14 @@
                 def _():
                     pltpu.make_async_copy(src, dst, by_recv.at[y, j, kind]).start()
 
+    halo_back(0)
+    halo_back(1)
     pairs(out_of_slots, 5, 3, 3)
     send_home(range(0, 6), 0)
-    halo_back(0)
-    halo_back(1)
+    halo_back(2)
+    halo_back(3)
     pairs(out_of_slots, 8, 3, 3)
     send_home(range(6, 12), 0)
-    halo_back(2)
-    halo_back(3)
     merge(0)
     send_home(range(0, 4), 1)
     merge(1)
@@ -493,6 +478,22 @@
     merge(2)
     merge(3)
     send_home(range(4, 8), 1)
+
+    for copy in v_copies:
+        if copy is v_copies[2]:
+            copy.wait()
+        else:
+            copy.wait_recv()
+    for k in range(7):
+        pot_rows[BOX * k : BOX * k + BOX, :] = v_win[k].astype(F32)[0:BOX]
+    pot_rows[7 * BOX : 128, :] = jnp.zeros((128 - 7 * BOX, 1024), F32)
+
+    near_rows = pot_rows[...].astype(BF)
+    row_of = lax.broadcasted_iota(jnp.int32, (128, FRAME), 0)
+    for j in range(3):
+        select = (row_of == starts[pl.ds(LEFT // 8 + 3 * y + j, 1), :]).astype(F32).astype(BF)
+        local = lax.dot_general(select, near_rows, (((0,), (0,)), ((), ())), preferred_element_type=F32)
+        pot_own[8 * j : 8 * j + 8] = local.reshape(8, 4, 8, 1024)
 
     loads[2].wait()
     for which in range(2):

time: 65.9 us -> 65 us (0.986)
  Pallas kernels: 65.1 us -> 64.2 us
    pallas_call x1, Pallas kernels: 63.9 us -> 63 us  [on_device(): pl.pallas_call(exchange_kernel, out_shape=(pltpu.VMEM((FUN, 4, 8, 1024),...]
where the time goes in v5:
time: 65 us; the launch traced here: 64.8 us
  Pallas kernels  64.2 us (99%)
    pallas_call x1, Pallas kernels, on_device(): pl.pallas_call(exchange_kernel, out_shape=(pltpu.VMEM((FUN, 4, 8, 1024),...  63 us

profile of v5, /device:TPU:0, one launch (start us, length us, event | category | flops | bytes accessed | tf_op | source)
XLA Modules:
  0.0 64.8 jit_solution(8278775926089658693)
XLA Ops:
  0.6 63.0 %exchange.1 = (bf16[24,4,8,1024]{3,2,1,0:T(8,128)(2,1)S(1)}, f32[24,256]{1,0:T(8,128)S(1)}) custom-call(bf16[24,4,8,1024]{3,2,1,0:T(8,128)(2,1)} %bitcast.3, bf16[1024,1024]{1,0:T(8,128)(2,1)} %kinetic.1, f32[12,1024]{1,0:T(8,128)} %pot_hbm.1, s32[24,128]{1,0:T(8,128)} %bitcast.4), custom_call_target="tpu_custom_call" | custom-call | tf_op jit(solution)/shard_map/exchange/pallas_call | solution.py:575
  63.7 1.2 %write.1 = (bf16[24,4,8,1024]{3,2,1,0:T(8,128)(2,1)}, f32[24,256]{1,0:T(8,128)}) custom-call(bf16[24,4,8,1024]{3,2,1,0:T(8,128)(2,1)S(1)} %get-tuple-element.6.pieces, f32[24,256]{1,0:T(8,128)S(1)} %get-tuple-element.7.rows), custom_call_target="tpu_custom_call" | custom-call | tf_op jit(solution)/shard_map/write/pallas_call | solution.py:616

commit v6 on v5

--- a/solution.py
+++ b/solution.py
@@ -224,8 +224,8 @@
 
     def gram_step(step, carry):
         lo, hi = gram[LIVE, 0:128], gram[LIVE, 128:256]
-        for part in range(4):
-            slot = 4 * step + part
+        for part in range(8):
+            slot = 8 * step + part
             held = slots[slot]
             prod = lax.dot_general(held[LIVE], held, (((1,), (1,)), ((), ())), preferred_element_type=F32)
             same_lo, same_hi = same_box(slot)
@@ -235,7 +235,7 @@
         gram[LIVE, 128:256] = hi
         return carry
 
-    lax.fori_loop(0, SUP // 4, gram_step, 0)
+    lax.fori_loop(0, SUP // 8, gram_step, 0)
     scaled = gram[...] * VOLUME
     gram[...] = scaled
     high_part = scaled.astype(BF)
@@ -382,8 +382,8 @@
         v_copies.append(copy)
 
     def mix_step(step, carry):
-        for part in range(4):
-            slot = 4 * step + part
+        for part in range(8):
+            slot = 8 * step + part
             same_lo, same_hi = same_box(slot)
             mix = jnp.concatenate(
                 [jnp.where(same_lo, mixing[LIVE, 0:128], 0.0), jnp.where(same_hi, mixing[LIVE, 128:256], 0.0)], axis=1
@@ -391,7 +391,7 @@
             slots[slot, LIVE, :] = jnp.dot(mix, slots[slot], preferred_element_type=F32).astype(BF)
         return carry
 
-    lax.fori_loop(0, SUP // 4, mix_step, 0)
+    lax.fori_loop(0, SUP // 8, mix_step, 0)
 
     for copy in forwards:
         copy.wait_send()

time: 65 us -> 64.1 us (0.986)
  Pallas kernels: 64.2 us -> 63.4 us
    pallas_call x1, Pallas kernels: 63 us -> 62.2 us  [on_device(): pl.pallas_call(exchange_kernel, out_shape=(pltpu.VMEM((FUN, 4, 8, 1024),...]
where the time goes in v6:
time: 64.1 us; the launch traced here: 64 us
  Pallas kernels  63.4 us (99%)
    pallas_call x1, Pallas kernels, on_device(): pl.pallas_call(exchange_kernel, out_shape=(pltpu.VMEM((FUN, 4, 8, 1024),...  62.2 us

profile of v6, /device:TPU:0, one launch (start us, length us, event | category | flops | bytes accessed | tf_op | source)
XLA Modules:
  0.0 64.0 jit_solution(4688783321209167591)
XLA Ops:
  0.6 62.2 %exchange.1 = (bf16[24,4,8,1024]{3,2,1,0:T(8,128)(2,1)S(1)}, f32[24,256]{1,0:T(8,128)S(1)}) custom-call(bf16[24,4,8,1024]{3,2,1,0:T(8,128)(2,1)} %bitcast.3, bf16[1024,1024]{1,0:T(8,128)(2,1)} %kinetic.1, f32[12,1024]{1,0:T(8,128)} %pot_hbm.1, s32[24,128]{1,0:T(8,128)} %bitcast.4), custom_call_target="tpu_custom_call" | custom-call | tf_op jit(solution)/shard_map/exchange/pallas_call | solution.py:575
  62.8 1.2 %write.1 = (bf16[24,4,8,1024]{3,2,1,0:T(8,128)(2,1)}, f32[24,256]{1,0:T(8,128)}) custom-call(bf16[24,4,8,1024]{3,2,1,0:T(8,128)(2,1)S(1)} %get-tuple-element.6.pieces, f32[24,256]{1,0:T(8,128)S(1)} %get-tuple-element.7.rows), custom_call_target="tpu_custom_call" | custom-call | tf_op jit(solution)/shard_map/write/pallas_call | solution.py:616
